TPU v7x, 32 devices: a whole 2x2x4 slice. The times are simulated.
32 devices in a mesh: days: 2 (over y), chan: 8 (over z, x), win: 2 (over core).
Axes of the slice: x: 2, y: 2, z: 4, core: 2. Of those that a mesh axis runs over, the one named last changes fastest.
Arguments:
- records: bfloat16 [2048, 2, 3000], P(('days', 'chan'), 'win'), parts along dimension 0, may hold values from -6 to 6
- assign: int32 [1024], P('chan'), may hold values from 0 to 127, as said below
- plan: int32 [1], replicated, may hold values from 0 to 2
- seg_mask: int32 [16, 2], P(('days', 'chan'), 'win'), parts along dimension 0, may hold values 0 or 1
Outputs:
- correlations: float32 [2, 1024, 128, 64], P('days', 'chan', 'win'), parts along dimension 0
There are 2 independent parts, one for each index of `days`. A program takes and returns all parts, laid end to end along the dimension named above; an argument that names none is the same for every part. Nothing has to cross between parts.
Inputs may be any that keep to these rules, and one draw needn't show every extreme that they name: `assign`: each aligned group of 128 entries holds every number from 0 to 127 once.
All inputs are finite; a program needn't handle non-finite values. No bound on the sum of `seg_mask` on one device may be relied on, other than what follows from the above.
Results may differ from a plain program's by a relative error of at most 0.005.
Values may be sent and summed in bfloat16 or wider, within the bound.
No kernel may reach another device: no remote copies, remote signals or barrier semaphores. Data moves between devices by JAX's collectives and lax.ppermute only.
A program may use at most 64 MiB of HBM per device.

v0:
```python
import math

import jax
import jax.numpy as jnp
from jax import lax
from jax.sharding import PartitionSpec as P

LAGS = 64


def partner(block, axis, bit):
    count = lax.axis_size(axis)
    route = []
    for low in range(count):
        high = low | 1 << bit
        if high != low and high < count:
            route += [(low, high), (high, low)]
    return lax.ppermute(block, axis, route)


def body(records, assign, plan, seg_mask):
    chan_rows, seg_count, seg_len = records.shape
    slot_table = (assign[:, None] == jnp.arange(chan_rows, dtype=jnp.int32)[None, :]).astype(
        jnp.bfloat16
    )
    ordered = jnp.dot(
        slot_table,
        records.reshape(chan_rows, seg_count * seg_len),
        preferred_element_type=jnp.float32,
    )
    ordered = ordered.astype(jnp.bfloat16).reshape(chan_rows, seg_count, seg_len)
    mask_bf = seg_mask.reshape(seg_count).astype(jnp.bfloat16)
    mask_own = seg_mask.reshape(seg_count).astype(jnp.float32)
    own_masked = ordered * mask_bf[None, :, None]
    own_flat = own_masked.reshape(chan_rows, seg_count * seg_len)
    digit_count = lax.axis_size("chan").bit_length() - 1
    lag_half = LAGS // 2
    pattern = plan[0]
    moved_data = ordered
    moved_mask = mask_bf
    for bit_pos in range(digit_count):
        arrived = partner((ordered, mask_bf), "chan", bit_pos)
        taken = pattern == bit_pos
        moved_data = jnp.where(taken, arrived[0], moved_data)
        moved_mask = jnp.where(taken, arrived[1], moved_mask)
    partner_masked = moved_data * moved_mask[None, :, None]
    padded = jnp.pad(partner_masked, ((0, 0), (0, 0), (lag_half, lag_half)))

    def lag_group(lag_start):
        pieces = [
            lax.dynamic_slice_in_dim(padded, lag_start + offset, seg_len, 2) for offset in range(4)
        ]
        shifted = jnp.stack(pieces, 0).reshape(4 * chan_rows, seg_count * seg_len)
        return lax.dot_general(
            own_flat, shifted, (((1,), (1,)), ((), ())), preferred_element_type=jnp.float32
        )

    starts = jnp.arange(LAGS // 4, dtype=jnp.int32) * 4
    products = lax.map(lag_group, starts)
    products = products.reshape(LAGS // 4, chan_rows, 4, chan_rows)
    lag_terms = jnp.transpose(products, (1, 3, 0, 2)).reshape(chan_rows, chan_rows, LAGS)
    valid_local = jnp.sum(mask_own * moved_mask.astype(jnp.float32))
    valid_count = lax.psum(valid_local, "win")
    stacked = lax.psum_scatter(
        lag_terms.astype(jnp.bfloat16), "win", scatter_dimension=1, tiled=True
    ).astype(jnp.float32)
    normed = stacked / (jnp.maximum(valid_count, 1.0) * math.sqrt(seg_len))
    results = [normed]
    return jnp.stack(results, 0)


def solution(mesh):
    placed = (P(("days", "chan"), "win", None), P("chan"), P(), P(("days", "chan"), "win"))
    return jax.shard_map(
        body, mesh=mesh, in_specs=placed, out_specs=P("days", "chan", "win", None), check_vma=False
    )
```

profile of v0, /device:TPU:0, one launch (start us, length us, event | category | flops | bytes accessed | tf_op | source)
XLA Modules:
  0.0 341.8 jit_solution(13484458072979626458)
XLA Ops:
  9.0 3.0 collective-permute-start.2
  13.6 2.6 collective-permute-start
  16.2 12.3 %collective-permute-start.5 = (bf16[1]{0:T(256)(128)(2,1)}, bf16[1]{0:T(256)(128)(2,1)}, u32[]{:S(2)}, u32[]{:S(2)}) collective-permute-start(bf16[1]{0:T(256)(128)(2,1)} %bitcast.13), channel_id=1, source_target_pairs={{0,2},{2,0},{4,6},{6,4},{8,10},{10,8},{12,14},{14,12},{1,3},{3,1},... | collective-permute-start | bytes 14 | tf_op jit(solution)/shard_map/ppermute | solution.py:18
  28.5 17.8 %collective-permute-start.4 = (bf16[1]{0:T(256)(128)(2,1)}, bf16[1]{0:T(256)(128)(2,1)}, u32[]{:S(2)}, u32[]{:S(2)}) collective-permute-start(bf16[1]{0:T(256)(128)(2,1)} %bitcast.13), channel_id=1, source_target_pairs={{0,4},{4,0},{2,6},{6,2},{8,12},{12,8},{10,14},{14,10},{1,5},{5,1},... | collective-permute-start | bytes 14 | tf_op jit(solution)/shard_map/ppermute | solution.py:18
  47.3 2.7 collective-permute-start.3
  54.2 264.2 %while.12 = (s32[]{:T(128)}, bf16[16,128,512]{1,2,0:T(8,128)(2,1)}, s32[16]{0:T(128)S(1)}, bf16[128,1,3064]{0,2,1:T(8,128)(2,1)S(1)}, bf16[128,3000]{1,0:T(8,128...) while((s32[]{:T(128)}, bf16[16,128,512]{1,2,0:T(8,128)(2,1)}, ...), condition=%wide.region_1.2_spmd, body=%wide.region_0.1_spmd.sunk | while | flops 397824000 | bytes 22608208 | solution.py:59
  60.7 1.9 pad_maximum_fusion.2
  62.5 4.7 %copy.14 = bf16[4,128,1,3000]{3,1,0,2:T(8,128)(2,1)} copy(bf16[4,128,1,3000]{1,3,2,0:T(8,128)(2,1)} %pad_maximum_fusion.2) | data formatting | bytes 6144000 | tf_op jit(solution)/shard_map/while/body/eval_jaxpr/stack | solution.py:53
  67.2 3.5 %fusion.10 = bf16[16,128,512]{1,2,0:T(8,128)(2,1)} fusion(bf16[16,128,512]{1,2,0:T(8,128)(2,1)} %get-tuple-element.157, s32[]{:T(128)S(6)} %copy.18, bf16[512,3000]{1,0:T(8,128)(2,1)} %bitcast.51, bf16[128,3000]{1,0:T(8,128)(2,1)S(1)} %get-tuple-element.173), kind=kOutput, calls=%fused_computation.2.clone.1 | convolution fusion | flops 393216000 | bytes 4175876 | tf_op jit(solution)/shard_map/while/body/eval_jaxpr/dot_general | solution.py:54
  77.2 1.9 pad_maximum_fusion.2
  79.1 4.7 %copy.14 = bf16[4,128,1,3000]{3,1,0,2:T(8,128)(2,1)} copy(bf16[4,128,1,3000]{1,3,2,0:T(8,128)(2,1)} %pad_maximum_fusion.2) | data formatting | bytes 6144000 | tf_op jit(solution)/shard_map/while/body/eval_jaxpr/stack | solution.py:53
  83.7 3.5 %fusion.10 = bf16[16,128,512]{1,2,0:T(8,128)(2,1)} fusion(bf16[16,128,512]{1,2,0:T(8,128)(2,1)} %get-tuple-element.157, s32[]{:T(128)S(6)} %copy.18, bf16[512,3000]{1,0:T(8,128)(2,1)} %bitcast.51, bf16[128,3000]{1,0:T(8,128)(2,1)S(1)} %get-tuple-element.173), kind=kOutput, calls=%fused_computation.2.clone.1 | convolution fusion | flops 393216000 | bytes 4175876 | tf_op jit(solution)/shard_map/while/body/eval_jaxpr/dot_general | solution.py:54
  93.7 1.9 pad_maximum_fusion.2
  95.6 4.7 %copy.14 = bf16[4,128,1,3000]{3,1,0,2:T(8,128)(2,1)} copy(bf16[4,128,1,3000]{1,3,2,0:T(8,128)(2,1)} %pad_maximum_fusion.2) | data formatting | bytes 6144000 | tf_op jit(solution)/shard_map/while/body/eval_jaxpr/stack | solution.py:53
  100.3 3.5 %fusion.10 = bf16[16,128,512]{1,2,0:T(8,128)(2,1)} fusion(bf16[16,128,512]{1,2,0:T(8,128)(2,1)} %get-tuple-element.157, s32[]{:T(128)S(6)} %copy.18, bf16[512,3000]{1,0:T(8,128)(2,1)} %bitcast.51, bf16[128,3000]{1,0:T(8,128)(2,1)S(1)} %get-tuple-element.173), kind=kOutput, calls=%fused_computation.2.clone.1 | convolution fusion | flops 393216000 | bytes 4175876 | tf_op jit(solution)/shard_map/while/body/eval_jaxpr/dot_general | solution.py:54
  112.1 4.7 %copy.14 = bf16[4,128,1,3000]{3,1,0,2:T(8,128)(2,1)} copy(bf16[4,128,1,3000]{1,3,2,0:T(8,128)(2,1)} %pad_maximum_fusion.2) | data formatting | bytes 6144000 | tf_op jit(solution)/shard_map/while/body/eval_jaxpr/stack | solution.py:53
  116.8 3.5 %fusion.10 = bf16[16,128,512]{1,2,0:T(8,128)(2,1)} fusion(bf16[16,128,512]{1,2,0:T(8,128)(2,1)} %get-tuple-element.157, s32[]{:T(128)S(6)} %copy.18, bf16[512,3000]{1,0:T(8,128)(2,1)} %bitcast.51, bf16[128,3000]{1,0:T(8,128)(2,1)S(1)} %get-tuple-element.173), kind=kOutput, calls=%fused_computation.2.clone.1 | convolution fusion | flops 393216000 | bytes 4175876 | tf_op jit(solution)/shard_map/while/body/eval_jaxpr/dot_general | solution.py:54
  126.7 1.9 pad_maximum_fusion.2
  128.6 4.7 %copy.14 = bf16[4,128,1,3000]{3,1,0,2:T(8,128)(2,1)} copy(bf16[4,128,1,3000]{1,3,2,0:T(8,128)(2,1)} %pad_maximum_fusion.2) | data formatting | bytes 6144000 | tf_op jit(solution)/shard_map/while/body/eval_jaxpr/stack | solution.py:53
  133.3 3.5 %fusion.10 = bf16[16,128,512]{1,2,0:T(8,128)(2,1)} fusion(bf16[16,128,512]{1,2,0:T(8,128)(2,1)} %get-tuple-element.157, s32[]{:T(128)S(6)} %copy.18, bf16[512,3000]{1,0:T(8,128)(2,1)} %bitcast.51, bf16[128,3000]{1,0:T(8,128)(2,1)S(1)} %get-tuple-element.173), kind=kOutput, calls=%fused_computation.2.clone.1 | convolution fusion | flops 393216000 | bytes 4175876 | tf_op jit(solution)/shard_map/while/body/eval_jaxpr/dot_general | solution.py:54
  145.1 4.7 %copy.14 = bf16[4,128,1,3000]{3,1,0,2:T(8,128)(2,1)} copy(bf16[4,128,1,3000]{1,3,2,0:T(8,128)(2,1)} %pad_maximum_fusion.2) | data formatting | bytes 6144000 | tf_op jit(solution)/shard_map/while/body/eval_jaxpr/stack | solution.py:53
  149.8 3.5 %fusion.10 = bf16[16,128,512]{1,2,0:T(8,128)(2,1)} fusion(bf16[16,128,512]{1,2,0:T(8,128)(2,1)} %get-tuple-element.157, s32[]{:T(128)S(6)} %copy.18, bf16[512,3000]{1,0:T(8,128)(2,1)} %bitcast.51, bf16[128,3000]{1,0:T(8,128)(2,1)S(1)} %get-tuple-element.173), kind=kOutput, calls=%fused_computation.2.clone.1 | convolution fusion | flops 393216000 | bytes 4175876 | tf_op jit(solution)/shard_map/while/body/eval_jaxpr/dot_general | solution.py:54
  161.6 4.7 %copy.14 = bf16[4,128,1,3000]{3,1,0,2:T(8,128)(2,1)} copy(bf16[4,128,1,3000]{1,3,2,0:T(8,128)(2,1)} %pad_maximum_fusion.2) | data formatting | bytes 6144000 | tf_op jit(solution)/shard_map/while/body/eval_jaxpr/stack | solution.py:53
  166.3 3.5 %fusion.10 = bf16[16,128,512]{1,2,0:T(8,128)(2,1)} fusion(bf16[16,128,512]{1,2,0:T(8,128)(2,1)} %get-tuple-element.157, s32[]{:T(128)S(6)} %copy.18, bf16[512,3000]{1,0:T(8,128)(2,1)} %bitcast.51, bf16[128,3000]{1,0:T(8,128)(2,1)S(1)} %get-tuple-element.173), kind=kOutput, calls=%fused_computation.2.clone.1 | convolution fusion | flops 393216000 | bytes 4175876 | tf_op jit(solution)/shard_map/while/body/eval_jaxpr/dot_general | solution.py:54
  178.1 4.7 %copy.14 = bf16[4,128,1,3000]{3,1,0,2:T(8,128)(2,1)} copy(bf16[4,128,1,3000]{1,3,2,0:T(8,128)(2,1)} %pad_maximum_fusion.2) | data formatting | bytes 6144000 | tf_op jit(solution)/shard_map/while/body/eval_jaxpr/stack | solution.py:53
  182.8 3.5 %fusion.10 = bf16[16,128,512]{1,2,0:T(8,128)(2,1)} fusion(bf16[16,128,512]{1,2,0:T(8,128)(2,1)} %get-tuple-element.157, s32[]{:T(128)S(6)} %copy.18, bf16[512,3000]{1,0:T(8,128)(2,1)} %bitcast.51, bf16[128,3000]{1,0:T(8,128)(2,1)S(1)} %get-tuple-element.173), kind=kOutput, calls=%fused_computation.2.clone.1 | convolution fusion | flops 393216000 | bytes 4175876 | tf_op jit(solution)/shard_map/while/body/eval_jaxpr/dot_general | solution.py:54
  194.7 4.7 %copy.14 = bf16[4,128,1,3000]{3,1,0,2:T(8,128)(2,1)} copy(bf16[4,128,1,3000]{1,3,2,0:T(8,128)(2,1)} %pad_maximum_fusion.2) | data formatting | bytes 6144000 | tf_op jit(solution)/shard_map/while/body/eval_jaxpr/stack | solution.py:53
  199.3 3.5 %fusion.10 = bf16[16,128,512]{1,2,0:T(8,128)(2,1)} fusion(bf16[16,128,512]{1,2,0:T(8,128)(2,1)} %get-tuple-element.157, s32[]{:T(128)S(6)} %copy.18, bf16[512,3000]{1,0:T(8,128)(2,1)} %bitcast.51, bf16[128,3000]{1,0:T(8,128)(2,1)S(1)} %get-tuple-element.173), kind=kOutput, calls=%fused_computation.2.clone.1 | convolution fusion | flops 393216000 | bytes 4175876 | tf_op jit(solution)/shard_map/while/body/eval_jaxpr/dot_general | solution.py:54
  211.2 4.7 %copy.14 = bf16[4,128,1,3000]{3,1,0,2:T(8,128)(2,1)} copy(bf16[4,128,1,3000]{1,3,2,0:T(8,128)(2,1)} %pad_maximum_fusion.2) | data formatting | bytes 6144000 | tf_op jit(solution)/shard_map/while/body/eval_jaxpr/stack | solution.py:53
  215.9 3.5 %fusion.10 = bf16[16,128,512]{1,2,0:T(8,128)(2,1)} fusion(bf16[16,128,512]{1,2,0:T(8,128)(2,1)} %get-tuple-element.157, s32[]{:T(128)S(6)} %copy.18, bf16[512,3000]{1,0:T(8,128)(2,1)} %bitcast.51, bf16[128,3000]{1,0:T(8,128)(2,1)S(1)} %get-tuple-element.173), kind=kOutput, calls=%fused_computation.2.clone.1 | convolution fusion | flops 393216000 | bytes 4175876 | tf_op jit(solution)/shard_map/while/body/eval_jaxpr/dot_general | solution.py:54
  225.8 1.9 pad_maximum_fusion.2
  227.7 4.7 %copy.14 = bf16[4,128,1,3000]{3,1,0,2:T(8,128)(2,1)} copy(bf16[4,128,1,3000]{1,3,2,0:T(8,128)(2,1)} %pad_maximum_fusion.2) | data formatting | bytes 6144000 | tf_op jit(solution)/shard_map/while/body/eval_jaxpr/stack | solution.py:53
  232.4 3.5 %fusion.10 = bf16[16,128,512]{1,2,0:T(8,128)(2,1)} fusion(bf16[16,128,512]{1,2,0:T(8,128)(2,1)} %get-tuple-element.157, s32[]{:T(128)S(6)} %copy.18, bf16[512,3000]{1,0:T(8,128)(2,1)} %bitcast.51, bf16[128,3000]{1,0:T(8,128)(2,1)S(1)} %get-tuple-element.173), kind=kOutput, calls=%fused_computation.2.clone.1 | convolution fusion | flops 393216000 | bytes 4175876 | tf_op jit(solution)/shard_map/while/body/eval_jaxpr/dot_general | solution.py:54
  244.2 4.7 %copy.14 = bf16[4,128,1,3000]{3,1,0,2:T(8,128)(2,1)} copy(bf16[4,128,1,3000]{1,3,2,0:T(8,128)(2,1)} %pad_maximum_fusion.2) | data formatting | bytes 6144000 | tf_op jit(solution)/shard_map/while/body/eval_jaxpr/stack | solution.py:53
  248.9 3.5 %fusion.10 = bf16[16,128,512]{1,2,0:T(8,128)(2,1)} fusion(bf16[16,128,512]{1,2,0:T(8,128)(2,1)} %get-tuple-element.157, s32[]{:T(128)S(6)} %copy.18, bf16[512,3000]{1,0:T(8,128)(2,1)} %bitcast.51, bf16[128,3000]{1,0:T(8,128)(2,1)S(1)} %get-tuple-element.173), kind=kOutput, calls=%fused_computation.2.clone.1 | convolution fusion | flops 393216000 | bytes 4175876 | tf_op jit(solution)/shard_map/while/body/eval_jaxpr/dot_general | solution.py:54
  258.8 1.9 pad_maximum_fusion.2
  260.7 4.7 %copy.14 = bf16[4,128,1,3000]{3,1,0,2:T(8,128)(2,1)} copy(bf16[4,128,1,3000]{1,3,2,0:T(8,128)(2,1)} %pad_maximum_fusion.2) | data formatting | bytes 6144000 | tf_op jit(solution)/shard_map/while/body/eval_jaxpr/stack | solution.py:53
  265.4 3.5 %fusion.10 = bf16[16,128,512]{1,2,0:T(8,128)(2,1)} fusion(bf16[16,128,512]{1,2,0:T(8,128)(2,1)} %get-tuple-element.157, s32[]{:T(128)S(6)} %copy.18, bf16[512,3000]{1,0:T(8,128)(2,1)} %bitcast.51, bf16[128,3000]{1,0:T(8,128)(2,1)S(1)} %get-tuple-element.173), kind=kOutput, calls=%fused_computation.2.clone.1 | convolution fusion | flops 393216000 | bytes 4175876 | tf_op jit(solution)/shard_map/while/body/eval_jaxpr/dot_general | solution.py:54
  277.2 4.7 %copy.14 = bf16[4,128,1,3000]{3,1,0,2:T(8,128)(2,1)} copy(bf16[4,128,1,3000]{1,3,2,0:T(8,128)(2,1)} %pad_maximum_fusion.2) | data formatting | bytes 6144000 | tf_op jit(solution)/shard_map/while/body/eval_jaxpr/stack | solution.py:53
  281.9 3.5 %fusion.10 = bf16[16,128,512]{1,2,0:T(8,128)(2,1)} fusion(bf16[16,128,512]{1,2,0:T(8,128)(2,1)} %get-tuple-element.157, s32[]{:T(128)S(6)} %copy.18, bf16[512,3000]{1,0:T(8,128)(2,1)} %bitcast.51, bf16[128,3000]{1,0:T(8,128)(2,1)S(1)} %get-tuple-element.173), kind=kOutput, calls=%fused_computation.2.clone.1 | convolution fusion | flops 393216000 | bytes 4175876 | tf_op jit(solution)/shard_map/while/body/eval_jaxpr/dot_general | solution.py:54
  293.7 4.7 %copy.14 = bf16[4,128,1,3000]{3,1,0,2:T(8,128)(2,1)} copy(bf16[4,128,1,3000]{1,3,2,0:T(8,128)(2,1)} %pad_maximum_fusion.2) | data formatting | bytes 6144000 | tf_op jit(solution)/shard_map/while/body/eval_jaxpr/stack | solution.py:53
  298.4 3.5 %fusion.10 = bf16[16,128,512]{1,2,0:T(8,128)(2,1)} fusion(bf16[16,128,512]{1,2,0:T(8,128)(2,1)} %get-tuple-element.157, s32[]{:T(128)S(6)} %copy.18, bf16[512,3000]{1,0:T(8,128)(2,1)} %bitcast.51, bf16[128,3000]{1,0:T(8,128)(2,1)S(1)} %get-tuple-element.173), kind=kOutput, calls=%fused_computation.2.clone.1 | convolution fusion | flops 393216000 | bytes 4175876 | tf_op jit(solution)/shard_map/while/body/eval_jaxpr/dot_general | solution.py:54
  310.2 4.7 %copy.14 = bf16[4,128,1,3000]{3,1,0,2:T(8,128)(2,1)} copy(bf16[4,128,1,3000]{1,3,2,0:T(8,128)(2,1)} %pad_maximum_fusion.2) | data formatting | bytes 6144000 | tf_op jit(solution)/shard_map/while/body/eval_jaxpr/stack | solution.py:53
  314.9 3.5 %fusion.10 = bf16[16,128,512]{1,2,0:T(8,128)(2,1)} fusion(bf16[16,128,512]{1,2,0:T(8,128)(2,1)} %get-tuple-element.157, s32[]{:T(128)S(6)} %copy.18, bf16[512,3000]{1,0:T(8,128)(2,1)} %bitcast.51, bf16[128,3000]{1,0:T(8,128)(2,1)S(1)} %get-tuple-element.173), kind=kOutput, calls=%fused_computation.2.clone.1 | convolution fusion | flops 393216000 | bytes 4175876 | tf_op jit(solution)/shard_map/while/body/eval_jaxpr/dot_general | solution.py:54
  318.5 4.6 %copy.12 = bf16[16,128,4,128]{1,2,0,3:T(4,128)(2,1)} copy(bf16[16,128,4,128]{1,3,2,0:T(8,128)(2,1)} %bitcast.56) | data formatting | bytes 4194304 | tf_op jit(solution)/shard_map/convert_element_type | solution.py:65
  323.1 3.6 %psum.7 = f32[]{:T(128)} all-reduce(f32[]{:T(128)} %bitcast.20), channel_id=1, replica_groups=mesh['days'=2,'chan'=8,'win'=2] {'win'}, use_global_device_ids=true, to_apply=%region_3.4 | all-reduce | flops 1 | bytes 8 | tf_op jit(solution)/shard_map/psum | solution.py:63
  327.3 4.8 %reduce-scatter.2.cloned.1.call-done = bf16[128,64,64]{0,2,1:T(8,128)(2,1)} async-done(((bf16[128,128,64]{0,2,1:T(8,128)(2,1)}), bf16[128,64,64]{0,2,1:T(8,128)(2,1)}) %reduce-scatter.2.cloned.1.call-update) | async-done | bytes 1048592 | tf_op jit(solution)/shard_map/reduce_scatter | solution.py:64
  332.1 2.8 divide_bitcast_fusion
  (59 shorter events, 46.7 us)
Async XLA Ops:
  6.5 1.1 copy-start
  6.5 325.6 %reduce-scatter.2.cloned.1.call-start = ((), (), s32[]{:S(2)}) async-start(), calls=%async_computation.1 | async-start | bytes 3145728 | tf_op jit(solution)/shard_map/reduce_scatter | solution.py:64
  9.0 43.6 %collective-permute-start.2 = (bf16[128,1,3000]{0,2,1:T(8,128)(2,1)S(1)}, bf16[128,1,3000]{0,2,1:T(8,128)(2,1)}, u32[]{:S(2)}, u32[]{:S(2)}) collective-permute-start(bf16[128,1,3000]{0,2,1:T(8,128)(2,1)S(1)} %bitcast.53), channel_id=1, source_target_pairs={{0,2},{2,0},{4,6},{6,4},{8,10},{10,8},{12,14},{14,12},{1,3},{3,1},... | collective-permute-start | bytes 2304008 | tf_op jit(solution)/shard_map/ppermute | solution.py:18
  12.0 40.5 %collective-permute-start.1 = (bf16[128,1,3000]{0,2,1:T(8,128)(2,1)S(1)}, bf16[128,1,3000]{0,2,1:T(8,128)(2,1)}, u32[]{:S(2)}, u32[]{:S(2)}) collective-permute-start(bf16[128,1,3000]{0,2,1:T(8,128)(2,1)S(1)} %bitcast.54), channel_id=1, source_target_pairs={{0,4},{4,0},{2,6},{6,2},{8,12},{12,8},{10,14},{14,10},{1,5},{5,1},... | collective-permute-start | bytes 2304008 | tf_op jit(solution)/shard_map/ppermute | solution.py:18
  13.6 39.0 %collective-permute-start = (bf16[128,1,3000]{0,2,1:T(8,128)(2,1)S(1)}, bf16[128,1,3000]{0,2,1:T(8,128)(2,1)}, u32[]{:S(2)}, u32[]{:S(2)}) collective-permute-start(bf16[128,1,3000]{0,2,1:T(8,128)(2,1)S(1)} %bitcast.55), channel_id=1, source_target_pairs={{0,8},{8,0},{2,10},{10,2},{4,12},{12,4},{6,14},{14,6},{1,9},{9,1},... | collective-permute-start | bytes 2304008 | tf_op jit(solution)/shard_map/ppermute | solution.py:18
  16.2 31.1 %collective-permute-start.5 = (bf16[1]{0:T(256)(128)(2,1)}, bf16[1]{0:T(256)(128)(2,1)}, u32[]{:S(2)}, u32[]{:S(2)}) collective-permute-start(bf16[1]{0:T(256)(128)(2,1)} %bitcast.13), channel_id=1, source_target_pairs={{0,2},{2,0},{4,6},{6,4},{8,10},{10,8},{12,14},{14,12},{1,3},{3,1},... | collective-permute-start | bytes 14 | tf_op jit(solution)/shard_map/ppermute | solution.py:18
  28.5 22.1 %collective-permute-start.4 = (bf16[1]{0:T(256)(128)(2,1)}, bf16[1]{0:T(256)(128)(2,1)}, u32[]{:S(2)}, u32[]{:S(2)}) collective-permute-start(bf16[1]{0:T(256)(128)(2,1)} %bitcast.13), channel_id=1, source_target_pairs={{0,4},{4,0},{2,6},{6,2},{8,12},{12,8},{10,14},{14,10},{1,5},{5,1},... | collective-permute-start | bytes 14 | tf_op jit(solution)/shard_map/ppermute | solution.py:18
  47.3 4.6 %collective-permute-start.3 = (bf16[1]{0:T(256)(128)(2,1)}, bf16[1]{0:T(256)(128)(2,1)}, u32[]{:S(2)}, u32[]{:S(2)}) collective-permute-start(bf16[1]{0:T(256)(128)(2,1)} %bitcast.13), channel_id=1, source_target_pairs={{0,8},{8,0},{2,10},{10,2},{4,12},{12,4},{6,14},{14,6},{1,9},{9,1},... | collective-permute-start | bytes 14 | tf_op jit(solution)/shard_map/ppermute | solution.py:18
Sparse Core Ops, SparseCore 0:
  323.2 8.9 reduce-scatter.1
where the time goes:
time: 345 us; the launch traced here: 342 us
  local copies, waits for them, and re-layouts  102 us (30%)
  loops' own time  80.9 us (23%)
  matrix products  57.7 us (17%)
  starting transfers between devices  39.9 us (12%)
  other arithmetic  34.3 us (10%)
  between operations  17.5 us (5%)
  waiting for transfers between devices  5.49 us (2%)
  blocking collectives  3.59 us (1%)
    another operation x32, local copies, waits for them, and re-layouts, lag_group(): shifted = jnp.stack(pieces, 0).reshape(4 * chan_rows, seg_count * seg_len)  87.9 us
    another operation x1, loops' own time, body(): products = lax.map(lag_group, starts)  80.9 us
    dot_general x16, matrix products, lag_group(): lax.dot_general(own_flat, shifted, (((1,), (1,)), ((), ())), preferred_el...  56.4 us
    ppermute x6, starting transfers between devices, partner(): return lax.ppermute(block, axis, route)  39.9 us
    another operation x16, other arithmetic, lag_group(): shifted = jnp.stack(pieces, 0).reshape(4 * chan_rows, seg_count * seg_len)  29.9 us
    dynamic_slice x16, local copies, waits for them, and re-layouts, body(): products = lax.map(lag_group, starts)  9.21 us
  transfers between devices with their start and end apart: 7, of which 2 were waited for; matrix products, arithmetic and copies ran while one was open for 0% of the time, Pallas kernels for 0%

commit v1 on v0

v1 whole, which is shorter than its diff:
```python
import jax
import jax.numpy as jnp
from jax import lax
from jax.experimental import pallas as pl
from jax.experimental.pallas import tpu as pltpu
from jax.sharding import PartitionSpec as P


LAGS = 64
HALF = LAGS // 2
GROUP = 16
BF16 = jnp.bfloat16
F32 = jnp.float32
PARAMS = pltpu.CompilerParams(vmem_limit_bytes=24 * 1024 * 1024)
SMEM = pl.BlockSpec(memory_space=pltpu.SMEM)
VMEM = pl.BlockSpec(memory_space=pltpu.VMEM)
ANY = pl.BlockSpec(memory_space=pl.ANY)


def picks(assign, mask, chans):
    source = lax.broadcasted_iota(jnp.int32, (chans, chans), 0)
    return jnp.where(source == assign, mask, 0.0)


def store_turned(rows, pad_ref, mask, out_refs):
    turned = lax.dot_general(
        rows.astype(BF16), pad_ref[...], (((1,), (1,)), ((), ())), preferred_element_type=F32
    )
    width = turned.shape[1]
    last = lax.broadcasted_iota(jnp.int32, (GROUP, 128), 1) == 127
    for at, out_ref in enumerate(out_refs):
        part = turned[at * GROUP : (at + 1) * GROUP]
        out_ref[:, pl.ds(0, width - 128)] = part[:, : width - 128].astype(BF16)
        out_ref[:, pl.ds(width - 128, 128)] = jnp.where(last, mask, part[:, width - 128 :]).astype(BF16)


def near_body(win_ref, mask_ref, rec_ref, assign_ref, *refs):
    out_refs = refs[:-4]
    pad_ref, pick_ref, slot_ref, sem = refs[-4:]
    seg_len, chans = rec_ref.shape
    width = pad_ref.shape[0]
    half = GROUP * len(out_refs)
    tail = width - HALF - seg_len
    load = pltpu.make_async_copy(rec_ref, pad_ref.at[pl.ds(HALF, seg_len)], sem.at[0])
    slots = pltpu.make_async_copy(assign_ref, slot_ref, sem.at[1])
    slots.start()
    load.start()
    pad_ref[pl.ds(0, HALF), :] = jnp.zeros((HALF, chans), BF16)
    pad_ref[pl.ds(HALF + seg_len, tail), :] = jnp.zeros((tail, chans), BF16)
    mask = mask_ref[0].astype(F32)
    slots.wait()
    pick_ref[...] = picks(slot_ref[...], mask, chans).T
    start = pl.multiple_of(win_ref[0] * half, half)
    rows = pick_ref[pl.ds(start, half), :]
    load.wait()
    store_turned(rows, pad_ref, mask, out_refs)


def far_body(win_ref, mask_ref, rec_ref, assign_ref, own_ref, *refs):
    out_refs = refs[:-4]
    pad_ref, pick_ref, slot_ref, sem = refs[-4:]
    seg_len, chans = rec_ref.shape
    width = pad_ref.shape[0]
    half = GROUP * len(out_refs)
    tail = width - HALF - seg_len
    load = pltpu.make_async_copy(rec_ref, pad_ref.at[pl.ds(HALF, seg_len)], sem.at[0])
    slots = pltpu.make_async_copy(assign_ref, slot_ref, sem.at[1])
    slots.start()
    load.start()
    pad_ref[pl.ds(0, HALF), :] = jnp.zeros((HALF, chans), BF16)
    pad_ref[pl.ds(HALF + seg_len, tail), :] = jnp.zeros((tail, chans), BF16)
    mask = mask_ref[0].astype(F32)
    slots.wait()
    pick = picks(slot_ref[...], mask, chans)
    pick_ref[...] = pick.T
    start = pl.multiple_of((1 - win_ref[0]) * half, half)
    rows = pick_ref[pl.ds(start, half), :]
    load.wait()
    store_turned(rows, pad_ref, mask, out_refs)
    ordered = jnp.dot(pad_ref[...], pick.astype(BF16), preferred_element_type=F32)
    own_ref[pl.ds(0, width), :] = ordered.astype(BF16)
    own_ref[pl.ds(width, HALF), :] = jnp.zeros((HALF, chans), BF16)
    own_ref[pl.ds(width + HALF, 16), :] = jnp.full((16, chans), mask, F32).astype(BF16)


def correlate(part_ref, own_ref, lhs_ref):
    part = part_ref[...]
    width = part.shape[1]
    for lag in range(HALF):
        moved = part if lag == 0 else pltpu.roll(part, width - lag, 1)
        lhs_ref[pl.ds(lag * GROUP, GROUP), :] = moved
    rhs = jnp.concatenate([own_ref[pl.ds(HALF, width), :], own_ref[pl.ds(0, width), :]], axis=1)
    return jnp.dot(lhs_ref[...], rhs, preferred_element_type=F32)


def first_body(own_ref, part_ref, term_ref, lhs_ref):
    term_ref[...] = correlate(part_ref, own_ref, lhs_ref).astype(BF16)


def second_body(at, mask_ref, own_ref, part_ref, near_ref, term_ref, *refs):
    out_ref, lhs_ref, done_ref, sem = refs[-4:]
    width = part_ref.shape[1]
    chans = own_ref.shape[1]
    seg_len = mask_ref[1].astype(F32)
    here = mask_ref[0].astype(F32) * near_ref[:, pl.ds(width - 1, 1)].astype(F32)
    there = own_ref[pl.ds(width + HALF, GROUP), pl.ds(0, 1)].astype(F32) * part_ref[
        :, pl.ds(width - 1, 1)
    ].astype(F32)
    scale = 1.0 / (jnp.maximum(here + there, 1.0) * jnp.sqrt(seg_len))
    scale = jnp.broadcast_to(scale, (GROUP, chans))
    terms = correlate(part_ref, own_ref, lhs_ref).astype(BF16).astype(F32)
    for lag in range(HALF):
        for high in range(2):
            rows = pl.ds(lag * GROUP, GROUP)
            lanes = pl.ds(high * chans, chans)
            mine = terms[lag * GROUP : (lag + 1) * GROUP, high * chans : (high + 1) * chans]
            total = (mine + term_ref[rows, lanes].astype(F32)) * scale
            done_ref[pl.ds(high * HALF + lag, GROUP, stride=LAGS), :] = total
    count = GROUP * LAGS
    store = pltpu.make_async_copy(done_ref, out_ref.at[pl.ds(at * count, count)], sem)
    store.start()
    store.wait()


def body(records, assign, plan, seg_mask):
    chans, seg_count, seg_len = records.shape
    blocks = lax.axis_size("chan")
    half = chans // lax.axis_size("win")
    groups = half // GROUP
    width = -(-(seg_len + LAGS) // 256) * 256
    win = lax.axis_index("win").astype(jnp.int32).reshape(1)
    mask = seg_mask.reshape(1)
    rec = records.reshape(chans, seg_count * seg_len).T
    slots = assign.reshape(1, chans)
    scalars = jnp.concatenate([mask, jnp.full((1,), seg_len, jnp.int32)])
    piece = jax.ShapeDtypeStruct((GROUP, width), BF16)
    prep_scratch = [
        pltpu.VMEM((width, chans), BF16),
        pltpu.VMEM((chans, chans), F32),
        pltpu.VMEM((1, chans), jnp.int32),
        pltpu.SemaphoreType.DMA((2,)),
    ]
    near_prep = pl.pallas_call(
        near_body,
        out_shape=(piece,) * groups,
        in_specs=[SMEM, SMEM, ANY, ANY],
        out_specs=(VMEM,) * groups,
        scratch_shapes=prep_scratch,
        compiler_params=PARAMS,
        cost_estimate=pl.CostEstimate(flops=1 << 26, bytes_accessed=1 << 20, transcendentals=0),
        name="near_prep",
    )
    own_shape = (width + HALF + 16, chans)
    far_prep = pl.pallas_call(
        far_body,
        out_shape=(jax.ShapeDtypeStruct(own_shape, BF16),) + (piece,) * groups,
        in_specs=[SMEM, SMEM, ANY, ANY],
        out_specs=(VMEM,) * (groups + 1),
        scratch_shapes=prep_scratch,
        compiler_params=PARAMS,
        cost_estimate=pl.CostEstimate(flops=1 << 27, bytes_accessed=1 << 20, transcendentals=0),
        name="far_prep",
    )
    rows = GROUP * HALF
    flops = 2 * rows * width * 2 * chans
    lhs = pltpu.VMEM((rows, width), BF16)
    first = pl.pallas_call(
        first_body,
        out_shape=jax.ShapeDtypeStruct((rows, 2 * chans), BF16),
        in_specs=[VMEM, VMEM],
        out_specs=VMEM,
        scratch_shapes=[lhs],
        compiler_params=PARAMS,
        cost_estimate=pl.CostEstimate(flops=flops, bytes_accessed=1 << 20, transcendentals=0),
        name="first",
    )
    total = jax.ShapeDtypeStruct((half * LAGS, chans), F32)

    def second(at):
        return pl.pallas_call(
            lambda *refs: second_body(at, *refs),
            out_shape=total,
            in_specs=[SMEM, VMEM, VMEM, VMEM, VMEM] + [ANY] * (at > 0),
            out_specs=ANY,
            scratch_shapes=[lhs, pltpu.VMEM((GROUP * LAGS, chans), F32), pltpu.SemaphoreType.DMA],
            input_output_aliases={5: 0} if at else {},
            compiler_params=PARAMS,
            cost_estimate=pl.CostEstimate(flops=flops, bytes_accessed=1 << 20, transcendentals=0),
            name="second",
        )

    def exchange(bit):
        straight = []
        crossed = []
        for low in range(blocks):
            for core in range(2):
                straight.append((low * 2 + core, (low ^ 1 << bit) * 2 + core))
                crossed.append((low * 2 + core, (low ^ 1 << bit) * 2 + 1 - core))

        def run(same):
            own, *cross = far_prep(win, mask, rec, slots)
            near = []
            for one in same:
                near.append(lax.ppermute(one, ("chan", "win"), straight))
            far = []
            for one in cross:
                far.append(lax.ppermute(one, ("chan", "win"), crossed))
            other = lax.ppermute(own, "win", [(0, 1), (1, 0)])
            out = ()
            for at in range(groups):
                terms = first(own, near[at])
                out = (second(at)(scalars, other, far[at], near[at], terms, *out),)
            return out[0]

        return run

    digits = blocks.bit_length() - 1
    same = near_prep(win, mask, rec, slots)
    out = lax.switch(plan[0], [exchange(bit) for bit in range(digits)], same)
    return jnp.transpose(out.reshape(half, LAGS, chans), (2, 0, 1))[None]


def solution(mesh):
    placed = (P(("days", "chan"), "win", None), P("chan"), P(), P(("days", "chan"), "win"))
    return jax.shard_map(
        body, mesh=mesh, in_specs=placed, out_specs=P("days", "chan", "win", None), check_vma=False
    )
```

time: 345 us -> 36.5 us (0.11)
  local copies, waits for them, and re-layouts: 102 us -> 0 us
  loops' own time: 80.9 us -> 0.38 us
  matrix products: 57.7 us -> 0 us
  other arithmetic: 34.3 us -> 0.08 us
  starting transfers between devices: 39.9 us -> 8.49 us
  Pallas kernels: 0 us -> 19.6 us
  between operations: 17.5 us -> 1.51 us
  blocking collectives: 3.59 us -> 0 us
    another operation x32 -> x0, local copies, waits for them, and re-layouts: 87.9 us -> none  [lag_group(): shifted = jnp.stack(pieces, 0).reshape(4 * chan_rows, seg_count * seg_len)]
    another operation x1, loops' own time: 80.9 us -> 0.38 us  [body(): out = lax.switch(plan[0], [exchange(bit) for bit in range(digits)], same)]
    dot_general x17 -> x0, matrix products: 57.7 us -> none  [the longest x16 56.4 us: lag_group(): lax.dot_general(own_flat, shifted, (((1,), (1,)), ((), ())), preferred_el...]
    another operation x17 -> x0, other arithmetic: 32.7 us -> none  [the longest x16 29.9 us: lag_group(): shifted = jnp.stack(pieces, 0).reshape(4 * chan_rows, seg_count * seg_len)]
    ppermute x6 -> x9, starting transfers between devices: 39.9 us -> 8.49 us  [the longest x4 4.66 us: run(): near.append(lax.ppermute(one, ('chan', 'win'), straight))]
    pallas_call x0 -> x10, Pallas kernels: none -> 19.6 us  [the longest x4 11.4 us: run(): out = (second(at)(scalars, other, far[at], near[at], terms, *out),)]
    dynamic_slice x16 -> x0, local copies, waits for them, and re-layouts: 9.21 us -> none  [body(): products = lax.map(lag_group, starts)]
    ppermute x6 -> x9, waiting for transfers between devices: 0.63 us -> 6.12 us  [the longest x4 4.23 us: run(): near.append(lax.ppermute(one, ('chan', 'win'), straight))]
  transfers between devices with their start and end apart: 7 -> 9, of which waited for: 2 -> 4; matrix products, arithmetic and copies ran while one was open for 0% -> 0% of each run, Pallas kernels for 0% -> 35%
where the time goes in v1:
time: 36.5 us; the launch traced here: 36.2 us
  Pallas kernels  19.6 us (54%)
  starting transfers between devices  8.49 us (23%)
  waiting for transfers between devices  6.12 us (17%)
  between operations  1.51 us (4%)
  loops' own time  0.38 us (1%)
    pallas_call x4, Pallas kernels, run(): out = (second(at)(scalars, other, far[at], near[at], terms, *out),)  11.4 us
    ppermute x4, starting transfers between devices, run(): near.append(lax.ppermute(one, ('chan', 'win'), straight))  4.66 us
    pallas_call x4, Pallas kernels, run(): terms = first(own, near[at])  4.31 us
    ppermute x4, waiting for transfers between devices, run(): near.append(lax.ppermute(one, ('chan', 'win'), straight))  4.23 us
    ppermute x4, starting transfers between devices, run(): far.append(lax.ppermute(one, ('chan', 'win'), crossed))  3.27 us
    pallas_call x1, Pallas kernels, run(): own, *cross = far_prep(win, mask, rec, slots)  2.42 us
    ppermute x4, waiting for transfers between devices, run(): far.append(lax.ppermute(one, ('chan', 'win'), crossed))  1.88 us
    pallas_call x1, Pallas kernels, body(): same = near_prep(win, mask, rec, slots)  1.55 us
  transfers between devices with their start and end apart: 9, of which 4 were waited for; matrix products, arithmetic and copies ran while one was open for 0% of the time, Pallas kernels for 35%

profile of v1, /device:TPU:0, one launch (start us, length us, event | category | flops | bytes accessed | tf_op | source)
XLA Modules:
  0.0 36.2 jit_solution(122577928407472575)
XLA Ops:
  1.3 0.1 pad_add_fusion
  1.4 1.5 %near_prep.1 = (bf16[16,3072]{1,0:T(8,128)(2,1)S(1)}, bf16[16,3072]{1,0:T(8,128)(2,1)S(1)}, bf16[16,3072]{1,0:T(8,128)(2,1)S(1)}, bf16[16,3072]{1,0:T(8,128)(2,1)S(1)}) custom-call(s32[1]{0:T(128)} %bitcast.1.win_ref, s32[1]{0:T(128)} %bitcast.12.mask_ref, bf16[3000,128]{1,0:T(8,128)(2,1)} %bitcast.14, s32[1,128]{1,0:T(1,128)} %bitcast.18), custom_call_target="tpu_custom_call" | custom-call | flops 67108864 | bytes 1048576 | tf_op jit(solution)/shard_map/near_prep/pallas_call | solution.py:218
  2.9 33.1 %conditional.1 = (f32[4096,128]{1,0:T(8,128)}) conditional(s32[]{:T(128)} %bitcast, (s32[1]{0:T(128)}, s32[1]{0:T(128)}, bf16[3000,128]{1,0:T(8,128)(2,1)}, s32[1,128]{1,0:T(1,128)}, bf16[16,3072]{1,0:T(8,128)(2,1)S(1)}, /*index=5*/bf16[16,3072]{1,0:T(8,128)(2,1)S(1)}, bf16[16,3072]{1,0:T(8,128)(2,1)S(1)}, ...), branch_computations={%region_0.0_spmd, %region_1.0_spmd, %region_2.0_spmd} | conditional | flops 6576668672 | bytes 15778160 | solution.py:219
  2.9 2.4 %far_prep.3 = (bf16[3120,128]{1,0:T(8,128)(2,1)S(1)}, bf16[16,3072]{1,0:T(8,128)(2,1)S(1)}, bf16[16,3072]{1,0:T(8,128)(2,1)S(1)}, bf16[16,3072]{1,0:T(8,128)(2,1)S(1)}, bf16[16,3072]{1,0:T(8,128)(2,1)S(1)}) custom-call(s32[1]{0:T(128)} %get-tuple-element.64.win_ref, s32[1]{0:T(128)} %get-tuple-element.65.mask_ref, ...), custom_call_target="tpu_custom_call" | custom-call | flops 134217728 | bytes 1048576 | tf_op jit(solution)/shard_map/cond/branch_0_fun/far_prep/pallas_call | solution.py:201
  5.4 0.6 %collective-permute-start = (bf16[3120,128]{1,0:T(8,128)(2,1)S(1)}, bf16[3120,128]{1,0:T(8,128)(2,1)S(1)}, u32[]{:S(2)}, u32[]{:S(2)}) collective-permute-start(bf16[3120,128]{1,0:T(8,128)(2,1)S(1)} %get-tuple-element.68.own_ref), channel_id=1, source_target_pairs={{0,1},{1,0},{2,3},{3,2},{4,5},{5,4},{6,7},{7,6},{8,9},{9,8},{10,11... | collective-permute-start | bytes 2396168 | tf_op jit(solution)/shard_map/cond/branch_0_fun/ppermute | solution.py:208
  5.9 2.6 %collective-permute-start.8 = (bf16[16,3072]{1,0:T(8,128)(2,1)S(1)}, bf16[16,3072]{1,0:T(8,128)(2,1)S(1)}, u32[]{:S(2)}, u32[]{:S(2)}) collective-permute-start(bf16[16,3072]{1,0:T(8,128)(2,1)S(1)} %get-tuple-element.76), channel_id=1, source_target_pairs={{0,2},{1,3},{2,0},{3,1},{4,6},{5,7},{6,4},{7,5},{8,10},{9,11},{10,... | collective-permute-start | bytes 294920 | tf_op jit(solution)/shard_map/cond/branch_0_fun/ppermute | solution.py:204
  8.5 0.1 collective-permute-start.6
  8.6 1.9 %collective-permute-start.2 = (bf16[16,3072]{1,0:T(8,128)(2,1)S(1)}, bf16[16,3072]{1,0:T(8,128)(2,1)S(1)}, u32[]{:S(2)}, u32[]{:S(2)}) collective-permute-start(bf16[16,3072]{1,0:T(8,128)(2,1)S(1)} %get-tuple-element.70), channel_id=1, source_target_pairs={{0,2},{1,3},{2,0},{3,1},{4,6},{5,7},{6,4},{7,5},{8,10},{9,11},{10,... | collective-permute-start | bytes 294920 | tf_op jit(solution)/shard_map/cond/branch_0_fun/ppermute | solution.py:204
  10.5 0.1 collective-permute-start.4
  10.6 1.5 %collective-permute-done.8.part_ref.refs_3_ = bf16[16,3072]{1,0:T(8,128)(2,1)S(1)} collective-permute-done((bf16[16,3072]{1,0:T(8,128)(2,1)S(1)}, bf16[16,3072]{1,0:T(8,128)(2,1)S(1)}, u32[]{:S(2)}, u32[]{:S(2)}) %collective-permute-start.8) | collective-permute-done | bytes 98336 | tf_op jit(solution)/shard_map/cond/branch_0_fun/ppermute | solution.py:204
  12.1 0.7 %collective-permute-start.1 = (bf16[16,3072]{1,0:T(8,128)(2,1)S(1)}, bf16[16,3072]{1,0:T(8,128)(2,1)S(1)}, u32[]{:S(2)}, u32[]{:S(2)}) collective-permute-start(bf16[16,3072]{1,0:T(8,128)(2,1)S(1)} %get-tuple-element.69), channel_id=1, source_target_pairs={{0,3},{1,2},{2,1},{3,0},{4,7},{5,6},{6,5},{7,4},{8,11},{9,10},{10,... | collective-permute-start | bytes 294920 | tf_op jit(solution)/shard_map/cond/branch_0_fun/ppermute | solution.py:207
  12.8 1.1 %first.15.refs_4_ = bf16[512,256]{1,0:T(8,128)(2,1)S(1)} custom-call(bf16[3120,128]{1,0:T(8,128)(2,1)S(1)} %get-tuple-element.68.own_ref, bf16[16,3072]{1,0:T(8,128)(2,1)S(1)} %collective-permute-done.8.part_ref.refs_3_), custom_call_target="tpu_custom_call" | custom-call | flops 805306368 | bytes 1048576 | tf_op jit(solution)/shard_map/cond/branch_0_fun/first/pallas_call | solution.py:211
  13.9 0.4 collective-permute-done.6.part_ref.refs_3_
  14.2 0.8 %collective-permute-start.3 = (bf16[16,3072]{1,0:T(8,128)(2,1)S(1)}, bf16[16,3072]{1,0:T(8,128)(2,1)S(1)}, u32[]{:S(2)}, u32[]{:S(2)}) collective-permute-start(bf16[16,3072]{1,0:T(8,128)(2,1)S(1)} %get-tuple-element.71), channel_id=1, source_target_pairs={{0,3},{1,2},{2,1},{3,0},{4,7},{5,6},{6,5},{7,4},{8,11},{9,10},{10,... | collective-permute-start | bytes 294920 | tf_op jit(solution)/shard_map/cond/branch_0_fun/ppermute | solution.py:207
  15.0 1.1 %first.14.refs_4_ = bf16[512,256]{1,0:T(8,128)(2,1)S(1)} custom-call(bf16[3120,128]{1,0:T(8,128)(2,1)S(1)} %get-tuple-element.68.own_ref, bf16[16,3072]{1,0:T(8,128)(2,1)S(1)} %collective-permute-done.6.part_ref.refs_3_), custom_call_target="tpu_custom_call" | custom-call | flops 805306368 | bytes 1048576 | tf_op jit(solution)/shard_map/cond/branch_0_fun/first/pallas_call | solution.py:211
  16.1 2.3 %collective-permute-done.4.part_ref.refs_3_ = bf16[16,3072]{1,0:T(8,128)(2,1)S(1)} collective-permute-done((bf16[16,3072]{1,0:T(8,128)(2,1)S(1)}, bf16[16,3072]{1,0:T(8,128)(2,1)S(1)}, u32[]{:S(2)}, u32[]{:S(2)}) %collective-permute-start.4) | collective-permute-done | bytes 98336 | tf_op jit(solution)/shard_map/cond/branch_0_fun/ppermute | solution.py:204
  18.5 0.7 %collective-permute-start.7 = (bf16[16,3072]{1,0:T(8,128)(2,1)S(1)}, bf16[16,3072]{1,0:T(8,128)(2,1)S(1)}, u32[]{:S(2)}, u32[]{:S(2)}) collective-permute-start(bf16[16,3072]{1,0:T(8,128)(2,1)S(1)} %get-tuple-element.75), channel_id=1, source_target_pairs={{0,3},{1,2},{2,1},{3,0},{4,7},{5,6},{6,5},{7,4},{8,11},{9,10},{10,... | collective-permute-start | bytes 294920 | tf_op jit(solution)/shard_map/cond/branch_0_fun/ppermute | solution.py:207
  19.1 1.1 %first.13.refs_4_ = bf16[512,256]{1,0:T(8,128)(2,1)S(1)} custom-call(bf16[3120,128]{1,0:T(8,128)(2,1)S(1)} %get-tuple-element.68.own_ref, bf16[16,3072]{1,0:T(8,128)(2,1)S(1)} %collective-permute-done.4.part_ref.refs_3_), custom_call_target="tpu_custom_call" | custom-call | flops 805306368 | bytes 1048576 | tf_op jit(solution)/shard_map/cond/branch_0_fun/first/pallas_call | solution.py:211
  20.2 0.0 collective-permute-done.2.part_ref.refs_3_
  20.2 1.2 %collective-permute-start.5 = (bf16[16,3072]{1,0:T(8,128)(2,1)S(1)}, bf16[16,3072]{1,0:T(8,128)(2,1)S(1)}, u32[]{:S(2)}, u32[]{:S(2)}) collective-permute-start(bf16[16,3072]{1,0:T(8,128)(2,1)S(1)} %get-tuple-element.73), channel_id=1, source_target_pairs={{0,3},{1,2},{2,1},{3,0},{4,7},{5,6},{6,5},{7,4},{8,11},{9,10},{10,... | collective-permute-start | bytes 294920 | tf_op jit(solution)/shard_map/cond/branch_0_fun/ppermute | solution.py:207
  21.4 1.1 %first.12.refs_4_ = bf16[512,256]{1,0:T(8,128)(2,1)S(1)} custom-call(bf16[3120,128]{1,0:T(8,128)(2,1)S(1)} %get-tuple-element.68.own_ref, bf16[16,3072]{1,0:T(8,128)(2,1)S(1)} %collective-permute-done.2.part_ref.refs_3_), custom_call_target="tpu_custom_call" | custom-call | flops 805306368 | bytes 1048576 | tf_op jit(solution)/shard_map/cond/branch_0_fun/first/pallas_call | solution.py:211
  22.4 1.9 %collective-permute-done.7.refs_2_ = bf16[16,3072]{1,0:T(8,128)(2,1)S(1)} collective-permute-done((bf16[16,3072]{1,0:T(8,128)(2,1)S(1)}, bf16[16,3072]{1,0:T(8,128)(2,1)S(1)}, u32[]{:S(2)}, u32[]{:S(2)}) %collective-permute-start.7) | collective-permute-done | bytes 98336 | tf_op jit(solution)/shard_map/cond/branch_0_fun/ppermute | solution.py:207
  24.3 0.0 collective-permute-done.refs_1_
  24.3 2.8 %second.12.refs_5_ = f32[4096,128]{1,0:T(8,128)} custom-call(s32[2]{0:T(128)S(1)} %get-tuple-element.62.refs_0_, bf16[3120,128]{1,0:T(8,128)(2,1)S(1)} %collective-permute-done.refs_1_, bf16[16,3072]{1,0:T(8,128)(2,1)S(1)} %collective-permute-done.7.refs_2_, bf16[16,3072]{1,0:T(8,128)(2,1)S(1)} %collective-permute-done.8.part_ref.refs_3_, ...), custom_call_target="tpu_custom_call" | custom-call | flops 805306368 | bytes 1048576 | tf_op jit(solution)/shard_map/cond/branch_0_fun/second/pallas_call | solution.py:212
  27.2 0.0 collective-permute-done.5.refs_2_
  27.2 2.8 %second.13.refs_5_ = f32[4096,128]{1,0:T(8,128)} custom-call(s32[2]{0:T(128)S(1)} %get-tuple-element.62.refs_0_, bf16[3120,128]{1,0:T(8,128)(2,1)S(1)} %collective-permute-done.refs_1_, bf16[16,3072]{1,0:T(8,128)(2,1)S(1)} %collective-permute-done.5.refs_2_, ...), custom_call_target="tpu_custom_call", output_to_operand_aliasing={{}: (5, {})} | custom-call | flops 805306368 | bytes 1048576 | tf_op jit(solution)/shard_map/cond/branch_0_fun/second/pallas_call | solution.py:212
  30.0 0.0 collective-permute-done.3.refs_2_
  30.0 2.8 %second.14.refs_5_ = f32[4096,128]{1,0:T(8,128)} custom-call(s32[2]{0:T(128)S(1)} %get-tuple-element.62.refs_0_, bf16[3120,128]{1,0:T(8,128)(2,1)S(1)} %collective-permute-done.refs_1_, bf16[16,3072]{1,0:T(8,128)(2,1)S(1)} %collective-permute-done.3.refs_2_, ...), custom_call_target="tpu_custom_call", output_to_operand_aliasing={{}: (5, {})} | custom-call | flops 805306368 | bytes 1048576 | tf_op jit(solution)/shard_map/cond/branch_0_fun/second/pallas_call | solution.py:212
  32.9 0.0 collective-permute-done.1.refs_2_
  32.9 2.8 %second.15 = f32[4096,128]{1,0:T(8,128)} custom-call(s32[2]{0:T(128)S(1)} %get-tuple-element.62.refs_0_, bf16[3120,128]{1,0:T(8,128)(2,1)S(1)} %collective-permute-done.refs_1_, bf16[16,3072]{1,0:T(8,128)(2,1)S(1)} %collective-permute-done.1.refs_2_, bf16[16,3072]{1,0:T(8,128)(2,1)S(1)} %collective-permute-done.2.part_ref.refs_3_, ...), custom_call_target="tpu_custom_call", output_to_operand_aliasing={{}: (5, {})} | custom-call | flops 805306368 | bytes 1048576 | tf_op jit(solution)/shard_map/cond/branch_0_fun/second/pallas_call | solution.py:212
Async XLA Ops:
  5.4 18.9 %collective-permute-start = (bf16[3120,128]{1,0:T(8,128)(2,1)S(1)}, bf16[3120,128]{1,0:T(8,128)(2,1)S(1)}, u32[]{:S(2)}, u32[]{:S(2)}) collective-permute-start(bf16[3120,128]{1,0:T(8,128)(2,1)S(1)} %get-tuple-element.68.own_ref), channel_id=1, source_target_pairs={{0,1},{1,0},{2,3},{3,2},{4,5},{5,4},{6,7},{7,6},{8,9},{9,8},{10,11... | collective-permute-start | bytes 2396168 | tf_op jit(solution)/shard_map/cond/branch_0_fun/ppermute | solution.py:208
  5.9 6.2 %collective-permute-start.8 = (bf16[16,3072]{1,0:T(8,128)(2,1)S(1)}, bf16[16,3072]{1,0:T(8,128)(2,1)S(1)}, u32[]{:S(2)}, u32[]{:S(2)}) collective-permute-start(bf16[16,3072]{1,0:T(8,128)(2,1)S(1)} %get-tuple-element.76), channel_id=1, source_target_pairs={{0,2},{1,3},{2,0},{3,1},{4,6},{5,7},{6,4},{7,5},{8,10},{9,11},{10,... | collective-permute-start | bytes 294920 | tf_op jit(solution)/shard_map/cond/branch_0_fun/ppermute | solution.py:204
  8.5 5.8 %collective-permute-start.6 = (bf16[16,3072]{1,0:T(8,128)(2,1)S(1)}, bf16[16,3072]{1,0:T(8,128)(2,1)S(1)}, u32[]{:S(2)}, u32[]{:S(2)}) collective-permute-start(bf16[16,3072]{1,0:T(8,128)(2,1)S(1)} %get-tuple-element.74), channel_id=1, source_target_pairs={{0,2},{1,3},{2,0},{3,1},{4,6},{5,7},{6,4},{7,5},{8,10},{9,11},{10,... | collective-permute-start | bytes 294920 | tf_op jit(solution)/shard_map/cond/branch_0_fun/ppermute | solution.py:204
  8.6 11.6 %collective-permute-start.2 = (bf16[16,3072]{1,0:T(8,128)(2,1)S(1)}, bf16[16,3072]{1,0:T(8,128)(2,1)S(1)}, u32[]{:S(2)}, u32[]{:S(2)}) collective-permute-start(bf16[16,3072]{1,0:T(8,128)(2,1)S(1)} %get-tuple-element.70), channel_id=1, source_target_pairs={{0,2},{1,3},{2,0},{3,1},{4,6},{5,7},{6,4},{7,5},{8,10},{9,11},{10,... | collective-permute-start | bytes 294920 | tf_op jit(solution)/shard_map/cond/branch_0_fun/ppermute | solution.py:204
  10.5 7.9 %collective-permute-start.4 = (bf16[16,3072]{1,0:T(8,128)(2,1)S(1)}, bf16[16,3072]{1,0:T(8,128)(2,1)S(1)}, u32[]{:S(2)}, u32[]{:S(2)}) collective-permute-start(bf16[16,3072]{1,0:T(8,128)(2,1)S(1)} %get-tuple-element.72), channel_id=1, source_target_pairs={{0,2},{1,3},{2,0},{3,1},{4,6},{5,7},{6,4},{7,5},{8,10},{9,11},{10,... | collective-permute-start | bytes 294920 | tf_op jit(solution)/shard_map/cond/branch_0_fun/ppermute | solution.py:204
  12.1 20.8 %collective-permute-start.1 = (bf16[16,3072]{1,0:T(8,128)(2,1)S(1)}, bf16[16,3072]{1,0:T(8,128)(2,1)S(1)}, u32[]{:S(2)}, u32[]{:S(2)}) collective-permute-start(bf16[16,3072]{1,0:T(8,128)(2,1)S(1)} %get-tuple-element.69), channel_id=1, source_target_pairs={{0,3},{1,2},{2,1},{3,0},{4,7},{5,6},{6,5},{7,4},{8,11},{9,10},{10,... | collective-permute-start | bytes 294920 | tf_op jit(solution)/shard_map/cond/branch_0_fun/ppermute | solution.py:207
  14.2 15.8 %collective-permute-start.3 = (bf16[16,3072]{1,0:T(8,128)(2,1)S(1)}, bf16[16,3072]{1,0:T(8,128)(2,1)S(1)}, u32[]{:S(2)}, u32[]{:S(2)}) collective-permute-start(bf16[16,3072]{1,0:T(8,128)(2,1)S(1)} %get-tuple-element.71), channel_id=1, source_target_pairs={{0,3},{1,2},{2,1},{3,0},{4,7},{5,6},{6,5},{7,4},{8,11},{9,10},{10,... | collective-permute-start | bytes 294920 | tf_op jit(solution)/shard_map/cond/branch_0_fun/ppermute | solution.py:207
  18.5 5.9 %collective-permute-start.7 = (bf16[16,3072]{1,0:T(8,128)(2,1)S(1)}, bf16[16,3072]{1,0:T(8,128)(2,1)S(1)}, u32[]{:S(2)}, u32[]{:S(2)}) collective-permute-start(bf16[16,3072]{1,0:T(8,128)(2,1)S(1)} %get-tuple-element.75), channel_id=1, source_target_pairs={{0,3},{1,2},{2,1},{3,0},{4,7},{5,6},{6,5},{7,4},{8,11},{9,10},{10,... | collective-permute-start | bytes 294920 | tf_op jit(solution)/shard_map/cond/branch_0_fun/ppermute | solution.py:207
  20.2 7.0 %collective-permute-start.5 = (bf16[16,3072]{1,0:T(8,128)(2,1)S(1)}, bf16[16,3072]{1,0:T(8,128)(2,1)S(1)}, u32[]{:S(2)}, u32[]{:S(2)}) collective-permute-start(bf16[16,3072]{1,0:T(8,128)(2,1)S(1)} %get-tuple-element.73), channel_id=1, source_target_pairs={{0,3},{1,2},{2,1},{3,0},{4,7},{5,6},{6,5},{7,4},{8,11},{9,10},{10,... | collective-permute-start | bytes 294920 | tf_op jit(solution)/shard_map/cond/branch_0_fun/ppermute | solution.py:207

commit v2 on v1

v2 whole, which is shorter than its diff:
```python
import math

import jax
import jax.numpy as jnp
from jax import lax
from jax.experimental import pallas as pl
from jax.experimental.pallas import tpu as pltpu
from jax.sharding import PartitionSpec as P


LAGS = 64
HALF = LAGS // 2
GROUP = 16
NEARS = 2
LOADS = 4
BF16 = jnp.bfloat16
F32 = jnp.float32
PARAMS = pltpu.CompilerParams(vmem_limit_bytes=24 * 1024 * 1024)

NEAR_PARAMS = pltpu.CompilerParams(vmem_limit_bytes=62 * 1024 * 1024)
SMEM = pl.BlockSpec(memory_space=pltpu.SMEM)
VMEM = pl.BlockSpec(memory_space=pltpu.VMEM)
ANY = pl.BlockSpec(memory_space=pl.ANY)
HBM = pl.BlockSpec(memory_space=pltpu.HBM)


def picks(assign, mask, chans):
    source = lax.broadcasted_iota(jnp.int32, (chans, chans), 0)
    return jnp.where(source == assign, mask, 0.0)


def store_turned(rows, pad_ref, mask, out_refs):
    turned = lax.dot_general(
        rows, pad_ref[...], (((1,), (1,)), ((), ())), preferred_element_type=F32
    )
    width = turned.shape[1]
    at = 0
    for out_ref in out_refs:
        count = out_ref.shape[0]
        last = lax.broadcasted_iota(jnp.int32, (count, 128), 1) == 127
        part = turned[at : at + count]
        at += count
        out_ref[:, pl.ds(0, width - 128)] = part[:, : width - 128].astype(BF16)
        out_ref[:, pl.ds(width - 128, 128)] = jnp.where(last, mask, part[:, width - 128 :]).astype(BF16)


def near_body(win_ref, mask_ref, rec_ref, assign_ref, *refs):
    out_refs = refs[:-7]
    pad_ref, far_ref, pick_ref, meta_ref, turn_ref, slot_ref, sem = refs[-7:]
    seg_len, chans = rec_ref.shape
    width = pad_ref.shape[0]
    half = chans // 2
    tail = width - HALF - seg_len
    slots = pltpu.make_async_copy(assign_ref, slot_ref, sem.at[LOADS])
    slots.start()
    cut = -(-seg_len // (8 * LOADS)) * 8
    loads = []
    for at in range(LOADS):
        count = min(cut, seg_len - at * cut)
        source = rec_ref.at[pl.ds(at * cut, count)]
        target = pad_ref.at[pl.ds(HALF + at * cut, count)]
        loads.append(pltpu.make_async_copy(source, target, sem.at[at]))
        loads[-1].start()
    pad_ref[pl.ds(0, HALF), :] = jnp.zeros((HALF, chans), BF16)
    pad_ref[pl.ds(HALF + seg_len, tail), :] = jnp.zeros((tail, chans), BF16)
    mask = mask_ref[0, 0].astype(F32)
    meta_ref[...] = jnp.full(meta_ref.shape, mask, F32)
    slots.wait()
    pick = picks(slot_ref[...], mask, chans)
    pick_ref[...] = pick.astype(BF16)
    turn_ref[...] = pick.T
    start = pl.multiple_of(win_ref[0] * half, half)
    other = pl.multiple_of((1 - win_ref[0]) * half, half)
    rows = turn_ref[pl.ds(start, half), :]
    far_ref[...] = turn_ref[pl.ds(other, half), :].astype(BF16)
    for load in loads:
        load.wait()
    store_turned(rows.astype(BF16), pad_ref, mask, out_refs)


def far_body(pad_ref, rows_ref, pick_ref, meta_ref, own_ref, *out_refs):
    width, chans = pad_ref.shape
    mask = meta_ref[pl.ds(0, 1), pl.ds(0, 1)]
    store_turned(rows_ref[...], pad_ref, mask, out_refs)
    ordered = jnp.dot(pad_ref[...], pick_ref[...], preferred_element_type=F32)
    own_ref[pl.ds(0, width), :] = ordered.astype(BF16)
    own_ref[pl.ds(width, HALF), :] = jnp.zeros((HALF, chans), BF16)
    own_ref[pl.ds(width + HALF, 16), :] = meta_ref[...].astype(BF16)


def correlate(part, own_ref, lhs_ref):
    width = part.shape[1]
    for lag in range(HALF):
        moved = part if lag == 0 else pltpu.roll(part, width - lag, 1)
        lhs_ref[pl.ds(lag * GROUP, GROUP), :] = moved
    rhs = jnp.concatenate([own_ref[pl.ds(HALF, width), :], own_ref[pl.ds(0, width), :]], axis=1)
    return jnp.dot(lhs_ref[...], rhs, preferred_element_type=F32)


def first_body(own_ref, part_ref, term_ref, lhs_ref):
    def step(at, carry):
        part = part_ref[pl.ds(pl.multiple_of(at * GROUP, GROUP), GROUP), :]
        terms = correlate(part, own_ref, lhs_ref).astype(BF16)
        term_ref[pl.ds(pl.multiple_of(at * GROUP * HALF, GROUP), GROUP * HALF), :] = terms
        return carry

    lax.fori_loop(0, part_ref.shape[0] // GROUP, step, 0)


def second_body(at, skip, seg_len, meta_ref, own_ref, part_ref, near_ref, term_ref, *refs):
    out_ref, lhs_ref, done_ref, sem = refs[-4:]
    width = part_ref.shape[1]
    chans = own_ref.shape[1]
    here = meta_ref[...] * near_ref[pl.ds(skip, GROUP), pl.ds(width - 128, 128)].astype(F32)
    there = own_ref[pl.ds(width + HALF, GROUP), :].astype(F32) * part_ref[
        :, pl.ds(width - 128, 128)
    ].astype(F32)
    count = (here + there)[:, 127:128]
    scale = 1.0 / (jnp.maximum(count, 1.0) * math.sqrt(seg_len))
    scale = jnp.broadcast_to(scale, (GROUP, chans))
    terms = correlate(part_ref[...], own_ref, lhs_ref).astype(BF16).astype(F32)
    stores = []
    slab = 8
    for low in range(0, GROUP, slab):
        for lag in range(HALF):
            for high in range(2):
                row = lag * GROUP + low
                lanes = pl.ds(high * chans, chans)
                mine = terms[row : row + slab, high * chans : (high + 1) * chans]
                held = term_ref[pl.ds(skip * HALF + row, slab), lanes].astype(F32)
                total = (mine + held) * scale[low : low + slab]
                done_ref[pl.ds(low * LAGS + high * HALF + lag, slab, stride=LAGS), :] = total
        source = done_ref.at[pl.ds(low * LAGS, slab * LAGS)]
        target = out_ref.at[pl.ds((at * GROUP + low) * LAGS, slab * LAGS)]
        stores.append(pltpu.make_async_copy(source, target, sem.at[low // slab]))
        stores[-1].start()
    for store in stores:
        store.wait()


def body(records, assign, plan, seg_mask):
    chans, seg_count, seg_len = records.shape
    blocks = lax.axis_size("chan")
    half = chans // lax.axis_size("win")
    groups = half // GROUP
    width = -(-(seg_len + LAGS) // 256) * 256
    win = lax.axis_index("win").astype(jnp.int32).reshape(1)
    rec = records.reshape(chans, seg_count * seg_len).T
    slots = assign.reshape(1, chans)
    per_near = half // NEARS
    shape = jax.ShapeDtypeStruct
    near_prep = pl.pallas_call(
        near_body,
        out_shape=(shape((per_near, width), BF16),) * NEARS
        + (shape((width, chans), BF16), shape((half, chans), BF16), shape((chans, chans), BF16))
        + (shape((16, 128), F32),),
        in_specs=[SMEM, SMEM, HBM, HBM],
        out_specs=(VMEM,) * (NEARS + 4),
        scratch_shapes=[
            pltpu.VMEM((chans, chans), F32),
            pltpu.VMEM((1, chans), jnp.int32),
            pltpu.SemaphoreType.DMA((LOADS + 1,)),
        ],
        compiler_params=NEAR_PARAMS,
        cost_estimate=pl.CostEstimate(flops=1 << 26, bytes_accessed=1 << 20, transcendentals=0),
        name="near_prep",
    )
    far_prep = pl.pallas_call(
        far_body,
        out_shape=(shape((width + HALF + 16, chans), BF16),) + (shape((GROUP, width), BF16),) * groups,
        in_specs=[VMEM] * 4,
        out_specs=(VMEM,) * (groups + 1),
        compiler_params=PARAMS,
        cost_estimate=pl.CostEstimate(flops=1 << 27, bytes_accessed=1 << 20, transcendentals=0),
        name="far_prep",
    )
    rows = GROUP * HALF
    flops = 2 * rows * width * 2 * chans
    lhs = pltpu.VMEM((rows, width), BF16)
    first = pl.pallas_call(
        first_body,
        out_shape=shape((per_near * HALF, 2 * chans), BF16),
        in_specs=[VMEM, VMEM],
        out_specs=VMEM,
        scratch_shapes=[lhs],
        compiler_params=PARAMS,
        cost_estimate=pl.CostEstimate(flops=2 * flops, bytes_accessed=1 << 20, transcendentals=0),
        name="first",
    )

    def second(at):
        skip = at * GROUP % per_near
        return pl.pallas_call(
            lambda *refs: second_body(at, skip, seg_len, *refs),
            out_shape=shape((half * LAGS, chans), F32),
            in_specs=[VMEM] * 5 + [ANY] * (at > 0),
            out_specs=ANY,
            scratch_shapes=[lhs, pltpu.VMEM((GROUP * LAGS, chans), F32), pltpu.SemaphoreType.DMA((2,))],
            input_output_aliases={5: 0} if at else {},
            compiler_params=PARAMS,
            cost_estimate=pl.CostEstimate(flops=flops, bytes_accessed=1 << 20, transcendentals=0),
            name="second",
        )

    def exchange(bit):
        straight = []
        crossed = []
        for low in range(blocks):
            for core in range(2):
                straight.append((low * 2 + core, (low ^ 1 << bit) * 2 + core))
                crossed.append((low * 2 + core, (low ^ 1 << bit) * 2 + 1 - core))

        def run(same, pad, turned, pick, meta):
            own, *cross = far_prep(pad, turned, pick, meta)
            near = []
            for one in same:
                near.append(lax.ppermute(one, ("chan", "win"), straight))
            far = []
            for one in cross:
                far.append(lax.ppermute(one, ("chan", "win"), crossed))
            other = lax.ppermute(own, "win", [(0, 1), (1, 0)])
            terms = [first(own, one) for one in near]
            out = ()
            for at in range(groups):
                side = at * GROUP // per_near
                out = (second(at)(meta, other, far[at], near[side], terms[side], *out),)
            return out[0]

        return run

    digits = blocks.bit_length() - 1
    *same, pad, turned, pick, meta = near_prep(win, seg_mask, rec, slots)
    branches = [exchange(bit) for bit in range(digits)]
    out = lax.switch(plan[0], branches, same, pad, turned, pick, meta)
    return jnp.transpose(out.reshape(half, LAGS, chans), (2, 0, 1))[None]


def solution(mesh):
    placed = (P(("days", "chan"), "win", None), P("chan"), P(), P(("days", "chan"), "win"))
    return jax.shard_map(
        body, mesh=mesh, in_specs=placed, out_specs=P("days", "chan", "win", None), check_vma=False
    )
```

time: 36.5 us -> 33.9 us (0.929)
  Pallas kernels: 19.6 us -> 15.2 us
  waiting for transfers between devices: 6.12 us -> 10.4 us
  starting transfers between devices: 8.49 us -> 6.26 us
    pallas_call x10 -> x8, Pallas kernels: 19.6 us -> 15.2 us  [the longest x4 8.61 us: run(): out = (second(at)(meta, other, far[at], near[side], terms[side], *out),)]
    ppermute x4, waiting for transfers between devices: 1.88 us -> 5.08 us  [run(): far.append(lax.ppermute(one, ('chan', 'win'), crossed))]
    ppermute x4 -> x2, starting transfers between devices: 4.66 us -> 2.64 us  [run(): near.append(lax.ppermute(one, ('chan', 'win'), straight))]
    ppermute x4 -> x2, waiting for transfers between devices: 4.23 us -> 5.3 us  [run(): near.append(lax.ppermute(one, ('chan', 'win'), straight))]
  transfers between devices with their start and end apart: 9 -> 7, of which waited for: 4 -> 3; matrix products, arithmetic and copies ran while one was open for 0% -> 0% of each run, Pallas kernels for 35% -> 32%
where the time goes in v2:
time: 33.9 us; the launch traced here: 33.7 us
  Pallas kernels  15.2 us (45%)
  waiting for transfers between devices  10.4 us (31%)
  starting transfers between devices  6.26 us (18%)
  between operations  1.51 us (4%)
  loops' own time  0.36 us (1%)
    pallas_call x4, Pallas kernels, run(): out = (second(at)(meta, other, far[at], near[side], terms[side], *out),)  8.61 us
    ppermute x2, waiting for transfers between devices, run(): near.append(lax.ppermute(one, ('chan', 'win'), straight))  5.3 us
    ppermute x4, waiting for transfers between devices, run(): far.append(lax.ppermute(one, ('chan', 'win'), crossed))  5.08 us
    pallas_call x2, Pallas kernels, run(): terms = [first(own, one) for one in near]  4.34 us
    ppermute x4, starting transfers between devices, run(): far.append(lax.ppermute(one, ('chan', 'win'), crossed))  3.07 us
    ppermute x2, starting transfers between devices, run(): near.append(lax.ppermute(one, ('chan', 'win'), straight))  2.64 us
    pallas_call x1, Pallas kernels, body(): *same, pad, turned, pick, meta = near_prep(win, seg_mask, rec, slots)  1.66 us
  transfers between devices with their start and end apart: 7, of which 3 were waited for; matrix products, arithmetic and copies ran while one was open for 0% of the time, Pallas kernels for 32%

profile of v2, /device:TPU:0, one launch (start us, length us, event | category | flops | bytes accessed | tf_op | source)
XLA Modules:
  0.0 33.7 jit_solution(182950484538233113)
XLA Ops:
  1.3 1.7 %near_prep.1 = (bf16[32,3072]{1,0:T(8,128)(2,1)S(1)}, bf16[32,3072]{1,0:T(8,128)(2,1)S(1)}, bf16[3072,128]{1,0:T(8,128)(2,1)S(1)}, bf16[64,128]{1,0:T(8,128)(2,1...) custom-call(s32[1]{0:T(128)} %bitcast.1.win_ref, s32[1,1]{1,0:T(1,128)S(6)} %copy.27.mask_ref, ...), custom_call_target="tpu_custom_call" | custom-call | flops 67108864 | bytes 1048576 | tf_op jit(solution)/shard_map/near_prep/pallas_call | solution.py:232
  3.0 30.6 %conditional.1 = (f32[4096,128]{1,0:T(8,128)}) conditional(s32[]{:T(128)} %bitcast, (bf16[3072,128]{1,0:T(8,128)(2,1)S(1)}, bf16[64,128]{1,0:T(8,128)(2,1)S(1)}, bf16[128,128]{1,0:T(8,128)(2,1)S(1)}, f32[16,128]{1,0:T(8,128)S(1)}, bf16[32,3072]{1,0:T(8,128)(2,1)S(1)}, /*index=5*/bf16[32,3072]{1,0:T(8,128)(2,1)S(1)}) %tuple.14, ...), branch_computations={%region_0.0_spmd, %region_1.0_spmd, %region_2.0_spmd} | conditional | flops 6576668672 | bytes 13680928 | solution.py:234
  3.0 0.6 %far_prep.3 = (bf16[3120,128]{1,0:T(8,128)(2,1)S(1)}, bf16[16,3072]{1,0:T(8,128)(2,1)S(1)}, bf16[16,3072]{1,0:T(8,128)(2,1)S(1)}, bf16[16,3072]{1,0:T(8,128)(2,1)S(1)}, bf16[16,3072]{1,0:T(8,128)(2,1)S(1)}) custom-call(bf16[3072,128]{1,0:T(8,128)(2,1)S(1)} %get-tuple-element.46.pad_ref, bf16[64,128]{1,0:T(8,128)(2,1)S(1)} %get-tuple-element.47.rows_ref, ...), custom_call_target="tpu_custom_call" | custom-call | flops 134217728 | bytes 1048576 | tf_op jit(solution)/shard_map/cond/branch_0_fun/far_prep/pallas_call | solution.py:214
  3.6 0.6 %collective-permute-start = (bf16[3120,128]{1,0:T(8,128)(2,1)S(1)}, bf16[3120,128]{1,0:T(8,128)(2,1)S(1)}, u32[]{:S(2)}, u32[]{:S(2)}) collective-permute-start(bf16[3120,128]{1,0:T(8,128)(2,1)S(1)} %get-tuple-element.49.own_ref), channel_id=1, source_target_pairs={{0,1},{1,0},{2,3},{3,2},{4,5},{5,4},{6,7},{7,6},{8,9},{9,8},{10,11... | collective-permute-start | bytes 2396168 | tf_op jit(solution)/shard_map/cond/branch_0_fun/ppermute | solution.py:221
  4.2 2.6 %collective-permute-start.5 = (bf16[32,3072]{1,0:T(8,128)(2,1)S(1)}, bf16[32,3072]{1,0:T(8,128)(2,1)S(1)}, u32[]{:S(2)}, u32[]{:S(2)}) collective-permute-start(bf16[32,3072]{1,0:T(8,128)(2,1)S(1)} %get-tuple-element.54), channel_id=1, source_target_pairs={{0,2},{1,3},{2,0},{3,1},{4,6},{5,7},{6,4},{7,5},{8,10},{9,11},{10,... | collective-permute-start | bytes 589832 | tf_op jit(solution)/shard_map/cond/branch_0_fun/ppermute | solution.py:217
  6.7 0.1 collective-permute-start.2
  6.8 1.4 %collective-permute-start.1 = (bf16[16,3072]{1,0:T(8,128)(2,1)S(1)}, bf16[16,3072]{1,0:T(8,128)(2,1)S(1)}, u32[]{:S(2)}, u32[]{:S(2)}) collective-permute-start(bf16[16,3072]{1,0:T(8,128)(2,1)S(1)} %get-tuple-element.50), channel_id=1, source_target_pairs={{0,3},{1,2},{2,1},{3,0},{4,7},{5,6},{6,5},{7,4},{8,11},{9,10},{10,... | collective-permute-start | bytes 294920 | tf_op jit(solution)/shard_map/cond/branch_0_fun/ppermute | solution.py:220
  8.2 0.3 collective-permute-start.3
  8.5 3.9 %collective-permute-done.5.part_ref.refs_3_ = bf16[32,3072]{1,0:T(8,128)(2,1)S(1)} collective-permute-done((bf16[32,3072]{1,0:T(8,128)(2,1)S(1)}, bf16[32,3072]{1,0:T(8,128)(2,1)S(1)}, u32[]{:S(2)}, u32[]{:S(2)}) %collective-permute-start.5) | collective-permute-done | bytes 196640 | tf_op jit(solution)/shard_map/cond/branch_0_fun/ppermute | solution.py:217
  12.5 0.7 %collective-permute-start.4 = (bf16[16,3072]{1,0:T(8,128)(2,1)S(1)}, bf16[16,3072]{1,0:T(8,128)(2,1)S(1)}, u32[]{:S(2)}, u32[]{:S(2)}) collective-permute-start(bf16[16,3072]{1,0:T(8,128)(2,1)S(1)} %get-tuple-element.53), channel_id=1, source_target_pairs={{0,3},{1,2},{2,1},{3,0},{4,7},{5,6},{6,5},{7,4},{8,11},{9,10},{10,... | collective-permute-start | bytes 294920 | tf_op jit(solution)/shard_map/cond/branch_0_fun/ppermute | solution.py:220
  13.1 2.2 %first.7.refs_4_ = bf16[1024,256]{1,0:T(8,128)(2,1)S(1)} custom-call(bf16[3120,128]{1,0:T(8,128)(2,1)S(1)} %get-tuple-element.49.own_ref, bf16[32,3072]{1,0:T(8,128)(2,1)S(1)} %collective-permute-done.5.part_ref.refs_3_), custom_call_target="tpu_custom_call" | custom-call | flops 1610612736 | bytes 1048576 | tf_op jit(solution)/shard_map/cond/branch_0_fun/first/pallas_call | solution.py:222
  15.3 1.4 %collective-permute-done.2.part_ref.refs_3_ = bf16[32,3072]{1,0:T(8,128)(2,1)S(1)} collective-permute-done((bf16[32,3072]{1,0:T(8,128)(2,1)S(1)}, bf16[32,3072]{1,0:T(8,128)(2,1)S(1)}, u32[]{:S(2)}, u32[]{:S(2)}) %collective-permute-start.2) | collective-permute-done | bytes 196640 | tf_op jit(solution)/shard_map/cond/branch_0_fun/ppermute | solution.py:217
  16.7 0.7 %collective-permute-start.6 = (bf16[16,3072]{1,0:T(8,128)(2,1)S(1)}, bf16[16,3072]{1,0:T(8,128)(2,1)S(1)}, u32[]{:S(2)}, u32[]{:S(2)}) collective-permute-start(bf16[16,3072]{1,0:T(8,128)(2,1)S(1)} %get-tuple-element.55), channel_id=1, source_target_pairs={{0,3},{1,2},{2,1},{3,0},{4,7},{5,6},{6,5},{7,4},{8,11},{9,10},{10,... | collective-permute-start | bytes 294920 | tf_op jit(solution)/shard_map/cond/branch_0_fun/ppermute | solution.py:220
  17.3 2.2 %first.6.refs_4_ = bf16[1024,256]{1,0:T(8,128)(2,1)S(1)} custom-call(bf16[3120,128]{1,0:T(8,128)(2,1)S(1)} %get-tuple-element.49.own_ref, bf16[32,3072]{1,0:T(8,128)(2,1)S(1)} %collective-permute-done.2.part_ref.refs_3_), custom_call_target="tpu_custom_call" | custom-call | flops 1610612736 | bytes 1048576 | tf_op jit(solution)/shard_map/cond/branch_0_fun/first/pallas_call | solution.py:222
  19.5 5.1 %collective-permute-done.6.refs_2_ = bf16[16,3072]{1,0:T(8,128)(2,1)S(1)} collective-permute-done((bf16[16,3072]{1,0:T(8,128)(2,1)S(1)}, bf16[16,3072]{1,0:T(8,128)(2,1)S(1)}, u32[]{:S(2)}, u32[]{:S(2)}) %collective-permute-start.6) | collective-permute-done | bytes 98336 | tf_op jit(solution)/shard_map/cond/branch_0_fun/ppermute | solution.py:220
  24.6 0.0 collective-permute-done.refs_1_
  24.6 2.1 %second.12.refs_5_ = f32[4096,128]{1,0:T(8,128)} custom-call(f32[16,128]{1,0:T(8,128)S(1)} %get-tuple-element.44.meta_ref.refs_0_, bf16[3120,128]{1,0:T(8,128)(2,1)S(1)} %collective-permute-done.refs_1_, bf16[16,3072]{1,0:T(8,128)(2,1)S(1)} %collective-permute-done.6.refs_2_, bf16[32,3072]{1,0:T(8,128)(2,1)S(1)} %collective-permute-done.5.part_ref.refs_3_, ...), custom_call_target="tpu_custom_call" | custom-call | flops 805306368 | bytes 1048576 | tf_op jit(solution)/shard_map/cond/branch_0_fun/second/pallas_call | solution.py:226
  26.8 0.0 collective-permute-done.4.refs_2_
  26.8 2.2 %second.13.refs_5_ = f32[4096,128]{1,0:T(8,128)} custom-call(f32[16,128]{1,0:T(8,128)S(1)} %get-tuple-element.44.meta_ref.refs_0_, bf16[3120,128]{1,0:T(8,128)(2,1)S(1)} %collective-permute-done.refs_1_, bf16[16,3072]{1,0:T(8,128)(2,1)S(1)} %collective-permute-done.4.refs_2_, ...), custom_call_target="tpu_custom_call", output_to_operand_aliasing={{}: (5, {})} | custom-call | flops 805306368 | bytes 1048576 | tf_op jit(solution)/shard_map/cond/branch_0_fun/second/pallas_call | solution.py:226
  28.9 0.0 collective-permute-done.3.refs_2_
  28.9 2.2 %second.14.refs_5_ = f32[4096,128]{1,0:T(8,128)} custom-call(f32[16,128]{1,0:T(8,128)S(1)} %get-tuple-element.44.meta_ref.refs_0_, bf16[3120,128]{1,0:T(8,128)(2,1)S(1)} %collective-permute-done.refs_1_, bf16[16,3072]{1,0:T(8,128)(2,1)S(1)} %collective-permute-done.3.refs_2_, ...), custom_call_target="tpu_custom_call", output_to_operand_aliasing={{}: (5, {})} | custom-call | flops 805306368 | bytes 1048576 | tf_op jit(solution)/shard_map/cond/branch_0_fun/second/pallas_call | solution.py:226
  31.1 0.0 collective-permute-done.1.refs_2_
  31.1 2.2 %second.15 = f32[4096,128]{1,0:T(8,128)} custom-call(f32[16,128]{1,0:T(8,128)S(1)} %get-tuple-element.44.meta_ref.refs_0_, bf16[3120,128]{1,0:T(8,128)(2,1)S(1)} %collective-permute-done.refs_1_, bf16[16,3072]{1,0:T(8,128)(2,1)S(1)} %collective-permute-done.1.refs_2_, ...), custom_call_target="tpu_custom_call", output_to_operand_aliasing={{}: (5, {})} | custom-call | flops 805306368 | bytes 1048576 | tf_op jit(solution)/shard_map/cond/branch_0_fun/second/pallas_call | solution.py:226
Async XLA Ops:
  3.6 21.0 %collective-permute-start = (bf16[3120,128]{1,0:T(8,128)(2,1)S(1)}, bf16[3120,128]{1,0:T(8,128)(2,1)S(1)}, u32[]{:S(2)}, u32[]{:S(2)}) collective-permute-start(bf16[3120,128]{1,0:T(8,128)(2,1)S(1)} %get-tuple-element.49.own_ref), channel_id=1, source_target_pairs={{0,1},{1,0},{2,3},{3,2},{4,5},{5,4},{6,7},{7,6},{8,9},{9,8},{10,11... | collective-permute-start | bytes 2396168 | tf_op jit(solution)/shard_map/cond/branch_0_fun/ppermute | solution.py:221
  4.2 8.3 %collective-permute-start.5 = (bf16[32,3072]{1,0:T(8,128)(2,1)S(1)}, bf16[32,3072]{1,0:T(8,128)(2,1)S(1)}, u32[]{:S(2)}, u32[]{:S(2)}) collective-permute-start(bf16[32,3072]{1,0:T(8,128)(2,1)S(1)} %get-tuple-element.54), channel_id=1, source_target_pairs={{0,2},{1,3},{2,0},{3,1},{4,6},{5,7},{6,4},{7,5},{8,10},{9,11},{10,... | collective-permute-start | bytes 589832 | tf_op jit(solution)/shard_map/cond/branch_0_fun/ppermute | solution.py:217
  6.7 10.0 %collective-permute-start.2 = (bf16[32,3072]{1,0:T(8,128)(2,1)S(1)}, bf16[32,3072]{1,0:T(8,128)(2,1)S(1)}, u32[]{:S(2)}, u32[]{:S(2)}) collective-permute-start(bf16[32,3072]{1,0:T(8,128)(2,1)S(1)} %get-tuple-element.51), channel_id=1, source_target_pairs={{0,2},{1,3},{2,0},{3,1},{4,6},{5,7},{6,4},{7,5},{8,10},{9,11},{10,... | collective-permute-start | bytes 589832 | tf_op jit(solution)/shard_map/cond/branch_0_fun/ppermute | solution.py:217
  6.8 24.3 %collective-permute-start.1 = (bf16[16,3072]{1,0:T(8,128)(2,1)S(1)}, bf16[16,3072]{1,0:T(8,128)(2,1)S(1)}, u32[]{:S(2)}, u32[]{:S(2)}) collective-permute-start(bf16[16,3072]{1,0:T(8,128)(2,1)S(1)} %get-tuple-element.50), channel_id=1, source_target_pairs={{0,3},{1,2},{2,1},{3,0},{4,7},{5,6},{6,5},{7,4},{8,11},{9,10},{10,... | collective-permute-start | bytes 294920 | tf_op jit(solution)/shard_map/cond/branch_0_fun/ppermute | solution.py:220
  8.2 20.7 %collective-permute-start.3 = (bf16[16,3072]{1,0:T(8,128)(2,1)S(1)}, bf16[16,3072]{1,0:T(8,128)(2,1)S(1)}, u32[]{:S(2)}, u32[]{:S(2)}) collective-permute-start(bf16[16,3072]{1,0:T(8,128)(2,1)S(1)} %get-tuple-element.52), channel_id=1, source_target_pairs={{0,3},{1,2},{2,1},{3,0},{4,7},{5,6},{6,5},{7,4},{8,11},{9,10},{10,... | collective-permute-start | bytes 294920 | tf_op jit(solution)/shard_map/cond/branch_0_fun/ppermute | solution.py:220
  12.5 14.3 %collective-permute-start.4 = (bf16[16,3072]{1,0:T(8,128)(2,1)S(1)}, bf16[16,3072]{1,0:T(8,128)(2,1)S(1)}, u32[]{:S(2)}, u32[]{:S(2)}) collective-permute-start(bf16[16,3072]{1,0:T(8,128)(2,1)S(1)} %get-tuple-element.53), channel_id=1, source_target_pairs={{0,3},{1,2},{2,1},{3,0},{4,7},{5,6},{6,5},{7,4},{8,11},{9,10},{10,... | collective-permute-start | bytes 294920 | tf_op jit(solution)/shard_map/cond/branch_0_fun/ppermute | solution.py:220
  16.7 7.9 %collective-permute-start.6 = (bf16[16,3072]{1,0:T(8,128)(2,1)S(1)}, bf16[16,3072]{1,0:T(8,128)(2,1)S(1)}, u32[]{:S(2)}, u32[]{:S(2)}) collective-permute-start(bf16[16,3072]{1,0:T(8,128)(2,1)S(1)} %get-tuple-element.55), channel_id=1, source_target_pairs={{0,3},{1,2},{2,1},{3,0},{4,7},{5,6},{6,5},{7,4},{8,11},{9,10},{10,... | collective-permute-start | bytes 294920 | tf_op jit(solution)/shard_map/cond/branch_0_fun/ppermute | solution.py:220

commit v3 on v2

--- a/solution.py
+++ b/solution.py
@@ -13,6 +13,7 @@
 GROUP = 16
 NEARS = 2
 LOADS = 4
+FARS = (16, 16, 16, 8, 8)
 BF16 = jnp.bfloat16
 F32 = jnp.float32
 PARAMS = pltpu.CompilerParams(vmem_limit_bytes=24 * 1024 * 1024)
@@ -89,15 +90,18 @@
 
 
 def correlate(part, own_ref, lhs_ref):
-    width = part.shape[1]
-    for lag in range(HALF):
-        moved = part if lag == 0 else pltpu.roll(part, width - lag, 1)
-        lhs_ref[pl.ds(lag * GROUP, GROUP), :] = moved
+    count, width = part.shape
+    pack = GROUP // count
+    for lag in range(0, HALF, pack):
+        moved = [part if step == 0 else pltpu.roll(part, width - step, 1) for step in range(lag, lag + pack)]
+        lhs_ref[pl.ds(lag * count, GROUP), :] = jnp.concatenate(moved, axis=0)
     rhs = jnp.concatenate([own_ref[pl.ds(HALF, width), :], own_ref[pl.ds(0, width), :]], axis=1)
     return jnp.dot(lhs_ref[...], rhs, preferred_element_type=F32)
 
 
-def first_body(own_ref, part_ref, term_ref, lhs_ref):
+def first_body(own_ref, part_ref, *refs):
+    term_ref, lhs_ref = refs[-2:]
+
     def step(at, carry):
         part = part_ref[pl.ds(pl.multiple_of(at * GROUP, GROUP), GROUP), :]
         terms = correlate(part, own_ref, lhs_ref).astype(BF16)
@@ -107,42 +111,51 @@
     lax.fori_loop(0, part_ref.shape[0] // GROUP, step, 0)
 
 
-def second_body(at, skip, seg_len, meta_ref, own_ref, part_ref, near_ref, term_ref, *refs):
-    out_ref, lhs_ref, done_ref, sem = refs[-4:]
-    width = part_ref.shape[1]
+def second_body(before, row, skip, final, seg_len, meta_ref, own_ref, part_ref, near_ref, term_ref, *refs):
+    lhs_ref, sem = refs[-2:]
+    count, width = part_ref.shape
     chans = own_ref.shape[1]
-    here = meta_ref[...] * near_ref[pl.ds(skip, GROUP), pl.ds(width - 128, 128)].astype(F32)
-    there = own_ref[pl.ds(width + HALF, GROUP), :].astype(F32) * part_ref[
+    outs = []
+    if before:
+        prior_ref = refs[0]
+        out_ref = refs[2] if row > before else refs[1]
+        target = out_ref.at[pl.ds((row - before) * LAGS, before * LAGS)]
+        outs.append(pltpu.make_async_copy(prior_ref, target, sem.at[0]))
+        outs[-1].start()
+    done_ref = refs[-3]
+    here = meta_ref[pl.ds(0, count), :] * near_ref[pl.ds(skip, count), pl.ds(width - 128, 128)].astype(F32)
+    there = own_ref[pl.ds(width + HALF, count), :].astype(F32) * part_ref[
         :, pl.ds(width - 128, 128)
     ].astype(F32)
-    count = (here + there)[:, 127:128]
-    scale = 1.0 / (jnp.maximum(count, 1.0) * math.sqrt(seg_len))
-    scale = jnp.broadcast_to(scale, (GROUP, chans))
+    valid = (here + there)[:, 127:128]
+    scale = 1.0 / (jnp.maximum(valid, 1.0) * math.sqrt(seg_len))
+    scale = jnp.broadcast_to(scale, (count, chans))
     terms = correlate(part_ref[...], own_ref, lhs_ref).astype(BF16).astype(F32)
-    stores = []
     slab = 8
-    for low in range(0, GROUP, slab):
+    for low in range(0, count, slab):
+        at = skip + low
+        held_at = at // GROUP * GROUP * HALF + at % GROUP
         for lag in range(HALF):
             for high in range(2):
-                row = lag * GROUP + low
                 lanes = pl.ds(high * chans, chans)
-                mine = terms[row : row + slab, high * chans : (high + 1) * chans]
-                held = term_ref[pl.ds(skip * HALF + row, slab), lanes].astype(F32)
+                line = lag * count + low
+                mine = terms[line : line + slab, high * chans : (high + 1) * chans]
+                held = term_ref[pl.ds(held_at + lag * GROUP, slab), lanes].astype(F32)
                 total = (mine + held) * scale[low : low + slab]
                 done_ref[pl.ds(low * LAGS + high * HALF + lag, slab, stride=LAGS), :] = total
-        source = done_ref.at[pl.ds(low * LAGS, slab * LAGS)]
-        target = out_ref.at[pl.ds((at * GROUP + low) * LAGS, slab * LAGS)]
-        stores.append(pltpu.make_async_copy(source, target, sem.at[low // slab]))
-        stores[-1].start()
-    for store in stores:
-        store.wait()
+        if final:
+            source = done_ref.at[pl.ds(low * LAGS, slab * LAGS)]
+            target = out_ref.at[pl.ds((row + low) * LAGS, slab * LAGS)]
+            outs.append(pltpu.make_async_copy(source, target, sem.at[1 + low // slab]))
+            outs[-1].start()
+    for out in outs:
+        out.wait()
 
 
 def body(records, assign, plan, seg_mask):
     chans, seg_count, seg_len = records.shape
     blocks = lax.axis_size("chan")
     half = chans // lax.axis_size("win")
-    groups = half // GROUP
     width = -(-(seg_len + LAGS) // 256) * 256
     win = lax.axis_index("win").astype(jnp.int32).reshape(1)
     rec = records.reshape(chans, seg_count * seg_len).T
@@ -167,9 +180,11 @@
     )
     far_prep = pl.pallas_call(
         far_body,
-        out_shape=(shape((width + HALF + 16, chans), BF16),) + (shape((GROUP, width), BF16),) * groups,
+        out_shape=(shape((width + HALF + 16, chans), BF16),) + tuple(
+            shape((count, width), BF16) for count in FARS
+        ),
         in_specs=[VMEM] * 4,
-        out_specs=(VMEM,) * (groups + 1),
+        out_specs=(VMEM,) * (len(FARS) + 1),
         compiler_params=PARAMS,
         cost_estimate=pl.CostEstimate(flops=1 << 27, bytes_accessed=1 << 20, transcendentals=0),
         name="far_prep",
@@ -177,29 +192,44 @@
     rows = GROUP * HALF
     flops = 2 * rows * width * 2 * chans
     lhs = pltpu.VMEM((rows, width), BF16)
-    first = pl.pallas_call(
-        first_body,
-        out_shape=shape((per_near * HALF, 2 * chans), BF16),
-        in_specs=[VMEM, VMEM],
-        out_specs=VMEM,
-        scratch_shapes=[lhs],
-        compiler_params=PARAMS,
-        cost_estimate=pl.CostEstimate(flops=2 * flops, bytes_accessed=1 << 20, transcendentals=0),
-        name="first",
-    )
-
-    def second(at):
-        skip = at * GROUP % per_near
+
+    def first(*args):
         return pl.pallas_call(
-            lambda *refs: second_body(at, skip, seg_len, *refs),
-            out_shape=shape((half * LAGS, chans), F32),
-            in_specs=[VMEM] * 5 + [ANY] * (at > 0),
-            out_specs=ANY,
-            scratch_shapes=[lhs, pltpu.VMEM((GROUP * LAGS, chans), F32), pltpu.SemaphoreType.DMA((2,))],
-            input_output_aliases={5: 0} if at else {},
+            first_body,
+            out_shape=shape((per_near * HALF, 2 * chans), BF16),
+            in_specs=[VMEM, VMEM] + [ANY] * (len(args) - 2),
+            out_specs=VMEM,
+            scratch_shapes=[lhs],
+            compiler_params=PARAMS,
+            cost_estimate=pl.CostEstimate(flops=2 * flops, bytes_accessed=1 << 20, transcendentals=0),
+            name="first",
+        )(*args)
+
+    def second(before, row, count):
+        skip = row % per_near
+        final = row + count == half
+        total = shape((half * LAGS, chans), F32)
+        done = shape((count * LAGS, chans), F32)
+        lines = pltpu.VMEM((count * HALF, width), BF16)
+        sems = pltpu.SemaphoreType.DMA((3,))
+        if final:
+            extra = dict(out_shape=(total,), out_specs=(ANY,))
+            scratch = [pltpu.VMEM(done.shape, F32), lines, sems]
+        elif before:
+            extra = dict(out_shape=(total, done), out_specs=(ANY, VMEM))
+            scratch = [lines, sems]
+        else:
+            extra = dict(out_shape=(done,), out_specs=(VMEM,))
+            scratch = [lines, sems]
+        return pl.pallas_call(
+            lambda *refs: second_body(before, row, skip, final, seg_len, *refs),
+            in_specs=[VMEM] * 5 + [VMEM] * (before > 0) + [ANY] * (row > before),
+            scratch_shapes=scratch,
+            input_output_aliases={6: 0} if row > before else {},
             compiler_params=PARAMS,
             cost_estimate=pl.CostEstimate(flops=flops, bytes_accessed=1 << 20, transcendentals=0),
             name="second",
+            **extra,
         )
 
     def exchange(bit):
@@ -219,11 +249,20 @@
             for one in cross:
                 far.append(lax.ppermute(one, ("chan", "win"), crossed))
             other = lax.ppermute(own, "win", [(0, 1), (1, 0)])
-            terms = [first(own, one) for one in near]
-            out = ()
-            for at in range(groups):
-                side = at * GROUP // per_near
-                out = (second(at)(meta, other, far[at], near[side], terms[side], *out),)
+            terms = []
+            for one in near:
+                terms.append(first(own, one, *terms[-1:]))
+            out = done = ()
+            before = row = 0
+            for one in far:
+                count = one.shape[0]
+                side = row // per_near
+                step = second(before, row, count)
+                result = step(meta, other, one, near[side], terms[side], *done, *out)
+                out = result[:1] if before else ()
+                done = result[-1:]
+                before = count
+                row += count
             return out[0]
 
         return run

time: 33.9 us -> 33.1 us (0.976)
  waiting for transfers between devices: 10.4 us -> 8.53 us
  starting transfers between devices: 6.26 us -> 7.7 us
  Pallas kernels: 15.2 us -> 14.8 us
    ppermute x4 -> x5, waiting for transfers between devices: 5.08 us -> 3.23 us  [run(): far.append(lax.ppermute(one, ('chan', 'win'), crossed))]
    ppermute x4 -> x5, starting transfers between devices: 3.07 us -> 4.5 us  [run(): far.append(lax.ppermute(one, ('chan', 'win'), crossed))]
    pallas_call x6 -> x7, Pallas kernels: 12.9 us -> 12.6 us  [the longest x5 8.22 us: run(): result = step(meta, other, one, near[side], terms[side], *done, *out)]
  transfers between devices with their start and end apart: 7 -> 8, of which waited for: 3 -> 4; matrix products, arithmetic and copies ran while one was open for 0% -> 0% of each run, Pallas kernels for 32% -> 32%
where the time goes in v3:
time: 33.1 us; the launch traced here: 32.9 us
  Pallas kernels  14.8 us (45%)
  waiting for transfers between devices  8.53 us (26%)
  starting transfers between devices  7.7 us (23%)
  between operations  1.51 us (5%)
  loops' own time  0.37 us (1%)
    pallas_call x5, Pallas kernels, run(): result = step(meta, other, one, near[side], terms[side], *done, *out)  8.22 us
    ppermute x2, waiting for transfers between devices, run(): near.append(lax.ppermute(one, ('chan', 'win'), straight))  5.3 us
    ppermute x5, starting transfers between devices, run(): far.append(lax.ppermute(one, ('chan', 'win'), crossed))  4.5 us
    pallas_call x2, Pallas kernels, first(): pl.pallas_call(first_body, out_shape=shape((per_near * HALF, 2 * chans),...  4.34 us
    ppermute x5, waiting for transfers between devices, run(): far.append(lax.ppermute(one, ('chan', 'win'), crossed))  3.23 us
    ppermute x2, starting transfers between devices, run(): near.append(lax.ppermute(one, ('chan', 'win'), straight))  2.64 us
    pallas_call x1, Pallas kernels, body(): *same, pad, turned, pick, meta = near_prep(win, seg_mask, rec, slots)  1.66 us
  transfers between devices with their start and end apart: 8, of which 4 were waited for; matrix products, arithmetic and copies ran while one was open for 0% of the time, Pallas kernels for 32%

profile of v3, /device:TPU:0, one launch (start us, length us, event | category | flops | bytes accessed | tf_op | source)
XLA Modules:
  0.0 32.9 jit_solution(10329024846873624836)
XLA Ops:
  1.3 1.7 %near_prep.1 = (bf16[32,3072]{1,0:T(8,128)(2,1)S(1)}, bf16[32,3072]{1,0:T(8,128)(2,1)S(1)}, bf16[3072,128]{1,0:T(8,128)(2,1)S(1)}, bf16[64,128]{1,0:T(8,128)(2,1...) custom-call(s32[1]{0:T(128)} %bitcast.1.win_ref, s32[1,1]{1,0:T(1,128)S(6)} %copy.27.mask_ref, ...), custom_call_target="tpu_custom_call" | custom-call | flops 67108864 | bytes 1048576 | tf_op jit(solution)/shard_map/near_prep/pallas_call | solution.py:271
  3.0 29.8 %conditional.1 = (f32[4096,128]{1,0:T(8,128)}) conditional(s32[]{:T(128)} %bitcast, (bf16[3072,128]{1,0:T(8,128)(2,1)S(1)}, bf16[64,128]{1,0:T(8,128)(2,1)S(1)}, bf16[128,128]{1,0:T(8,128)(2,1)S(1)}, f32[16,128]{1,0:T(8,128)S(1)}, bf16[32,3072]{1,0:T(8,128)(2,1)S(1)}, /*index=5*/bf16[32,3072]{1,0:T(8,128)(2,1)S(1)}) %tuple.14, ...), branch_computations={%region_0.0_spmd, %region_1.0_spmd, %region_2.0_spmd} | conditional | flops 7381975040 | bytes 14729544 | solution.py:273
  3.0 0.6 %far_prep.3 = (bf16[3120,128]{1,0:T(8,128)(2,1)S(1)}, bf16[16,3072]{1,0:T(8,128)(2,1)S(1)}, bf16[16,3072]{1,0:T(8,128)(2,1)S(1)}, bf16[16,3072]{1,0:T(8,128)(2,1...) custom-call(bf16[3072,128]{1,0:T(8,128)(2,1)S(1)} %get-tuple-element.46.pad_ref, ...), custom_call_target="tpu_custom_call" | custom-call | flops 134217728 | bytes 1048576 | tf_op jit(solution)/shard_map/cond/branch_0_fun/far_prep/pallas_call | solution.py:244
  3.6 0.6 %collective-permute-start = (bf16[3120,128]{1,0:T(8,128)(2,1)S(1)}, bf16[3120,128]{1,0:T(8,128)(2,1)S(1)}, u32[]{:S(2)}, u32[]{:S(2)}) collective-permute-start(bf16[3120,128]{1,0:T(8,128)(2,1)S(1)} %get-tuple-element.49.own_ref), channel_id=1, source_target_pairs={{0,1},{1,0},{2,3},{3,2},{4,5},{5,4},{6,7},{7,6},{8,9},{9,8},{10,11... | collective-permute-start | bytes 2396168 | tf_op jit(solution)/shard_map/cond/branch_0_fun/ppermute | solution.py:251
  4.2 2.6 %collective-permute-start.3 = (bf16[32,3072]{1,0:T(8,128)(2,1)S(1)}, bf16[32,3072]{1,0:T(8,128)(2,1)S(1)}, u32[]{:S(2)}, u32[]{:S(2)}) collective-permute-start(bf16[32,3072]{1,0:T(8,128)(2,1)S(1)} %get-tuple-element.52), channel_id=1, source_target_pairs={{0,2},{1,3},{2,0},{3,1},{4,6},{5,7},{6,4},{7,5},{8,10},{9,11},{10,... | collective-permute-start | bytes 589832 | tf_op jit(solution)/shard_map/cond/branch_0_fun/ppermute | solution.py:247
  6.7 0.1 collective-permute-start.2
  6.8 1.4 %collective-permute-start.1 = (bf16[8,3072]{1,0:T(8,128)(2,1)S(1)}, bf16[8,3072]{1,0:T(8,128)(2,1)S(1)}, u32[]{:S(2)}, u32[]{:S(2)}) collective-permute-start(bf16[8,3072]{1,0:T(8,128)(2,1)S(1)} %get-tuple-element.50), channel_id=1, source_target_pairs={{0,3},{1,2},{2,1},{3,0},{4,7},{5,6},{6,5},{7,4},{8,11},{9,10},{10,... | collective-permute-start | bytes 147464 | tf_op jit(solution)/shard_map/cond/branch_0_fun/ppermute | solution.py:250
  8.2 0.3 collective-permute-start.4
  8.5 3.9 %collective-permute-done.3.part_ref.refs_3_ = bf16[32,3072]{1,0:T(8,128)(2,1)S(1)} collective-permute-done((bf16[32,3072]{1,0:T(8,128)(2,1)S(1)}, bf16[32,3072]{1,0:T(8,128)(2,1)S(1)}, u32[]{:S(2)}, u32[]{:S(2)}) %collective-permute-start.3) | collective-permute-done | bytes 196640 | tf_op jit(solution)/shard_map/cond/branch_0_fun/ppermute | solution.py:247
  12.5 0.7 %collective-permute-start.6 = (bf16[16,3072]{1,0:T(8,128)(2,1)S(1)}, bf16[16,3072]{1,0:T(8,128)(2,1)S(1)}, u32[]{:S(2)}, u32[]{:S(2)}) collective-permute-start(bf16[16,3072]{1,0:T(8,128)(2,1)S(1)} %get-tuple-element.55), channel_id=1, source_target_pairs={{0,3},{1,2},{2,1},{3,0},{4,7},{5,6},{6,5},{7,4},{8,11},{9,10},{10,... | collective-permute-start | bytes 294920 | tf_op jit(solution)/shard_map/cond/branch_0_fun/ppermute | solution.py:250
  13.1 2.2 %first.6.refs_0_.refs_4_ = bf16[1024,256]{1,0:T(8,128)(2,1)S(1)} custom-call(bf16[3120,128]{1,0:T(8,128)(2,1)S(1)} %get-tuple-element.49.own_ref, bf16[32,3072]{1,0:T(8,128)(2,1)S(1)} %collective-permute-done.3.part_ref.refs_3_), custom_call_target="tpu_custom_call" | custom-call | flops 1610612736 | bytes 1048576 | tf_op jit(solution)/shard_map/cond/branch_0_fun/first/pallas_call | solution.py:197
  15.3 1.4 %collective-permute-done.2.part_ref.refs_3_ = bf16[32,3072]{1,0:T(8,128)(2,1)S(1)} collective-permute-done((bf16[32,3072]{1,0:T(8,128)(2,1)S(1)}, bf16[32,3072]{1,0:T(8,128)(2,1)S(1)}, u32[]{:S(2)}, u32[]{:S(2)}) %collective-permute-start.2) | collective-permute-done | bytes 196640 | tf_op jit(solution)/shard_map/cond/branch_0_fun/ppermute | solution.py:247
  16.7 0.7 %collective-permute-start.7 = (bf16[16,3072]{1,0:T(8,128)(2,1)S(1)}, bf16[16,3072]{1,0:T(8,128)(2,1)S(1)}, u32[]{:S(2)}, u32[]{:S(2)}) collective-permute-start(bf16[16,3072]{1,0:T(8,128)(2,1)S(1)} %get-tuple-element.56), channel_id=1, source_target_pairs={{0,3},{1,2},{2,1},{3,0},{4,7},{5,6},{6,5},{7,4},{8,11},{9,10},{10,... | collective-permute-start | bytes 294920 | tf_op jit(solution)/shard_map/cond/branch_0_fun/ppermute | solution.py:250
  17.3 2.2 %first.7.refs_4_ = bf16[1024,256]{1,0:T(8,128)(2,1)S(1)} custom-call(bf16[3120,128]{1,0:T(8,128)(2,1)S(1)} %get-tuple-element.49.own_ref, bf16[32,3072]{1,0:T(8,128)(2,1)S(1)} %collective-permute-done.2.part_ref.refs_3_, bf16[1024,256]{1,0:T(8,128)(2,1)S(1)} %first.6.refs_0_.refs_4_), custom_call_target="tpu_custom_call" | custom-call | flops 1610612736 | bytes 1048576 | tf_op jit(solution)/shard_map/cond/branch_0_fun/first/pallas_call | solution.py:197
  19.5 3.0 %collective-permute-done.7.refs_2_ = bf16[16,3072]{1,0:T(8,128)(2,1)S(1)} collective-permute-done((bf16[16,3072]{1,0:T(8,128)(2,1)S(1)}, bf16[16,3072]{1,0:T(8,128)(2,1)S(1)}, u32[]{:S(2)}, u32[]{:S(2)}) %collective-permute-start.7) | collective-permute-done | bytes 98336 | tf_op jit(solution)/shard_map/cond/branch_0_fun/ppermute | solution.py:250
  22.5 1.4 %collective-permute-start.5 = (bf16[16,3072]{1,0:T(8,128)(2,1)S(1)}, bf16[16,3072]{1,0:T(8,128)(2,1)S(1)}, u32[]{:S(2)}, u32[]{:S(2)}) collective-permute-start(bf16[16,3072]{1,0:T(8,128)(2,1)S(1)} %get-tuple-element.54), channel_id=1, source_target_pairs={{0,3},{1,2},{2,1},{3,0},{4,7},{5,6},{6,5},{7,4},{8,11},{9,10},{10,... | collective-permute-start | bytes 294920 | tf_op jit(solution)/shard_map/cond/branch_0_fun/ppermute | solution.py:250
  23.9 0.0 collective-permute-done.refs_1_
  23.9 1.5 %second.15.refs_5_ = f32[1024,128]{1,0:T(8,128)S(1)} custom-call(f32[16,128]{1,0:T(8,128)S(1)} %get-tuple-element.44.meta_ref.refs_0_, bf16[3120,128]{1,0:T(8,128)(2,1)S(1)} %collective-permute-done.refs_1_, bf16[16,3072]{1,0:T(8,128)(2,1)S(1)} %collective-permute-done.7.refs_2_, bf16[32,3072]{1,0:T(8,128)(2,1)S(1)} %collective-permute-done.3.part_ref.refs_3_, ...), custom_call_target="tpu_custom_call" | custom-call | flops 805306368 | bytes 1048576 | tf_op jit(solution)/shard_map/cond/branch_0_fun/second/pallas_call | solution.py:261
  25.4 0.0 collective-permute-done.6.refs_2_
  25.4 1.6 %second.16 = (f32[4096,128]{1,0:T(8,128)}, f32[1024,128]{1,0:T(8,128)S(1)}) custom-call(f32[16,128]{1,0:T(8,128)S(1)} %get-tuple-element.44.meta_ref.refs_0_, bf16[3120,128]{1,0:T(8,128)(2,1)S(1)} %collective-permute-done.refs_1_, bf16[16,3072]{1,0:T(8,128)(2,1)S(1)} %collective-permute-done.6.refs_2_, ...), custom_call_target="tpu_custom_call" | custom-call | flops 805306368 | bytes 1048576 | tf_op jit(solution)/shard_map/cond/branch_0_fun/second/pallas_call | solution.py:261
  27.0 0.3 collective-permute-done.5.refs_2_
  27.3 1.6 %second.17 = (f32[4096,128]{1,0:T(8,128)}, f32[1024,128]{1,0:T(8,128)S(1)}) custom-call(f32[16,128]{1,0:T(8,128)S(1)} %get-tuple-element.44.meta_ref.refs_0_, bf16[3120,128]{1,0:T(8,128)(2,1)S(1)} %collective-permute-done.refs_1_, bf16[16,3072]{1,0:T(8,128)(2,1)S(1)} %collective-permute-done.5.refs_2_, ...), custom_call_target="tpu_custom_call", output_to_operand_aliasing={{0}: (6, {})} | custom-call | flops 805306368 | bytes 1048576 | tf_op jit(solution)/shard_map/cond/branch_0_fun/second/pallas_call | solution.py:261
  28.9 0.0 collective-permute-done.4.refs_2_
  28.9 1.6 %second.18 = (f32[4096,128]{1,0:T(8,128)}, f32[512,128]{1,0:T(8,128)S(1)}) custom-call(f32[16,128]{1,0:T(8,128)S(1)} %get-tuple-element.44.meta_ref.refs_0_, bf16[3120,128]{1,0:T(8,128)(2,1)S(1)} %collective-permute-done.refs_1_, bf16[8,3072]{1,0:T(8,128)(2,1)S(1)} %collective-permute-done.4.refs_2_, ...), custom_call_target="tpu_custom_call", output_to_operand_aliasing={{0}: (6, {})} | custom-call | flops 805306368 | bytes 1048576 | tf_op jit(solution)/shard_map/cond/branch_0_fun/second/pallas_call | solution.py:261
  30.6 0.0 collective-permute-done.1.refs_2_
  30.6 1.9 %second.19 = f32[4096,128]{1,0:T(8,128)} custom-call(f32[16,128]{1,0:T(8,128)S(1)} %get-tuple-element.44.meta_ref.refs_0_, bf16[3120,128]{1,0:T(8,128)(2,1)S(1)} %collective-permute-done.refs_1_, bf16[8,3072]{1,0:T(8,128)(2,1)S(1)} %collective-permute-done.1.refs_2_, ...), custom_call_target="tpu_custom_call", output_to_operand_aliasing={{}: (6, {})} | custom-call | flops 805306368 | bytes 1048576 | tf_op jit(solution)/shard_map/cond/branch_0_fun/second/pallas_call | solution.py:261
Async XLA Ops:
  3.6 20.3 %collective-permute-start = (bf16[3120,128]{1,0:T(8,128)(2,1)S(1)}, bf16[3120,128]{1,0:T(8,128)(2,1)S(1)}, u32[]{:S(2)}, u32[]{:S(2)}) collective-permute-start(bf16[3120,128]{1,0:T(8,128)(2,1)S(1)} %get-tuple-element.49.own_ref), channel_id=1, source_target_pairs={{0,1},{1,0},{2,3},{3,2},{4,5},{5,4},{6,7},{7,6},{8,9},{9,8},{10,11... | collective-permute-start | bytes 2396168 | tf_op jit(solution)/shard_map/cond/branch_0_fun/ppermute | solution.py:251
  4.2 8.3 %collective-permute-start.3 = (bf16[32,3072]{1,0:T(8,128)(2,1)S(1)}, bf16[32,3072]{1,0:T(8,128)(2,1)S(1)}, u32[]{:S(2)}, u32[]{:S(2)}) collective-permute-start(bf16[32,3072]{1,0:T(8,128)(2,1)S(1)} %get-tuple-element.52), channel_id=1, source_target_pairs={{0,2},{1,3},{2,0},{3,1},{4,6},{5,7},{6,4},{7,5},{8,10},{9,11},{10,... | collective-permute-start | bytes 589832 | tf_op jit(solution)/shard_map/cond/branch_0_fun/ppermute | solution.py:247
  6.7 10.0 %collective-permute-start.2 = (bf16[32,3072]{1,0:T(8,128)(2,1)S(1)}, bf16[32,3072]{1,0:T(8,128)(2,1)S(1)}, u32[]{:S(2)}, u32[]{:S(2)}) collective-permute-start(bf16[32,3072]{1,0:T(8,128)(2,1)S(1)} %get-tuple-element.51), channel_id=1, source_target_pairs={{0,2},{1,3},{2,0},{3,1},{4,6},{5,7},{6,4},{7,5},{8,10},{9,11},{10,... | collective-permute-start | bytes 589832 | tf_op jit(solution)/shard_map/cond/branch_0_fun/ppermute | solution.py:247
  6.8 23.8 %collective-permute-start.1 = (bf16[8,3072]{1,0:T(8,128)(2,1)S(1)}, bf16[8,3072]{1,0:T(8,128)(2,1)S(1)}, u32[]{:S(2)}, u32[]{:S(2)}) collective-permute-start(bf16[8,3072]{1,0:T(8,128)(2,1)S(1)} %get-tuple-element.50), channel_id=1, source_target_pairs={{0,3},{1,2},{2,1},{3,0},{4,7},{5,6},{6,5},{7,4},{8,11},{9,10},{10,... | collective-permute-start | bytes 147464 | tf_op jit(solution)/shard_map/cond/branch_0_fun/ppermute | solution.py:250
  8.2 20.7 %collective-permute-start.4 = (bf16[8,3072]{1,0:T(8,128)(2,1)S(1)}, bf16[8,3072]{1,0:T(8,128)(2,1)S(1)}, u32[]{:S(2)}, u32[]{:S(2)}) collective-permute-start(bf16[8,3072]{1,0:T(8,128)(2,1)S(1)} %get-tuple-element.53), channel_id=1, source_target_pairs={{0,3},{1,2},{2,1},{3,0},{4,7},{5,6},{6,5},{7,4},{8,11},{9,10},{10,... | collective-permute-start | bytes 147464 | tf_op jit(solution)/shard_map/cond/branch_0_fun/ppermute | solution.py:250
  12.5 12.9 %collective-permute-start.6 = (bf16[16,3072]{1,0:T(8,128)(2,1)S(1)}, bf16[16,3072]{1,0:T(8,128)(2,1)S(1)}, u32[]{:S(2)}, u32[]{:S(2)}) collective-permute-start(bf16[16,3072]{1,0:T(8,128)(2,1)S(1)} %get-tuple-element.55), channel_id=1, source_target_pairs={{0,3},{1,2},{2,1},{3,0},{4,7},{5,6},{6,5},{7,4},{8,11},{9,10},{10,... | collective-permute-start | bytes 294920 | tf_op jit(solution)/shard_map/cond/branch_0_fun/ppermute | solution.py:250
  16.7 5.8 %collective-permute-start.7 = (bf16[16,3072]{1,0:T(8,128)(2,1)S(1)}, bf16[16,3072]{1,0:T(8,128)(2,1)S(1)}, u32[]{:S(2)}, u32[]{:S(2)}) collective-permute-start(bf16[16,3072]{1,0:T(8,128)(2,1)S(1)} %get-tuple-element.56), channel_id=1, source_target_pairs={{0,3},{1,2},{2,1},{3,0},{4,7},{5,6},{6,5},{7,4},{8,11},{9,10},{10,... | collective-permute-start | bytes 294920 | tf_op jit(solution)/shard_map/cond/branch_0_fun/ppermute | solution.py:250
  22.5 4.8 %collective-permute-start.5 = (bf16[16,3072]{1,0:T(8,128)(2,1)S(1)}, bf16[16,3072]{1,0:T(8,128)(2,1)S(1)}, u32[]{:S(2)}, u32[]{:S(2)}) collective-permute-start(bf16[16,3072]{1,0:T(8,128)(2,1)S(1)} %get-tuple-element.54), channel_id=1, source_target_pairs={{0,3},{1,2},{2,1},{3,0},{4,7},{5,6},{6,5},{7,4},{8,11},{9,10},{10,... | collective-permute-start | bytes 294920 | tf_op jit(solution)/shard_map/cond/branch_0_fun/ppermute | solution.py:250
